TPU v7x, 256 devices: a whole 4x4x8 slice. The times are simulated.
256 devices in a mesh: half: 2 (over core), dev: 128 (over y, x, z).
Axes of the slice: x: 4, y: 4, z: 8, core: 2. Of those that a mesh axis runs over, the one named last changes fastest.
Arguments:
- field_mix: float32 [32, 32], P('half'), may hold values from -1 to 1
- alm: bfloat16 [1024, 2, 32, 2048], P('dev', None, 'half'), may hold values from -6 to 6
- legendre: bfloat16 [1024, 2048, 128], P('dev'), may hold values from -0.125 to 0.125
- order_ids: int32 [1024], replicated, may hold values from 0 to 1023, each once
- fetch_list: int32 [128, 128, 2], replicated, may hold values from -1 to 31, as said below
- scan_tiles: int32 [512, 32], P('dev'), may hold values from 0 to 255, as said below
- block_tile: int32 [512, 32], P('dev'), may hold values from 0 to 31
- block_pix: int32 [512, 16384], P('dev'), may hold values from -1 to 127, as said below
- noise_kernel: float32 [512, 512], P('dev'), may hold values from -0.24 to 0.24
- scan_weight: float32 [512], P('dev'), may hold values from 0.1 to 1
Outputs:
- binned: float32 [128, 32, 4096], P('dev', 'half')
Inputs may be any that keep to these rules, and one draw needn't show every extreme that they name: `fetch_list`: entry [d, e, k] is the index, among the 32 tiles of device d, of the tile that device e fetches from d in slot k, or -1 for an empty slot; the live slots of one pair come first and name distinct tiles; every device fills all 2 slots from at least one source. `scan_tiles`: entry [n, i] is a slot source 2 + k whose fetch_list[source, n div 4, k] is not -1. `block_pix`: -1 marks a flagged sample.
All inputs are finite; a program needn't handle non-finite values.
Results may differ from a plain program's by a relative error of at most 0.007.
Values may be sent and summed in bfloat16 or wider, within the bound.
No kernel may reach another device: no remote copies, remote signals or barrier semaphores. Data moves between devices by JAX's collectives and lax.ppermute only.
A program may use at most 128 MiB of HBM per device.

v0:
```python
import math

import jax
import jax.numpy as jnp
from jax import lax
from jax.sharding import PartitionSpec as P

NPHI = 4096
TILE = 128
BLK = 512


def toeplitz_rows(band_values, block_len):
    scan_count = band_values.shape[0]
    wrapped = jnp.pad(band_values, ((0, 0), (0, 1)))
    repeated = jnp.tile(wrapped, (1, block_len))
    folded = repeated[:, : block_len * (2 * block_len - 1)].reshape(
        scan_count, block_len, 2 * block_len - 1
    )
    return folded[:, :, block_len - 1 :]


def local(
    field_mix,
    alm,
    legendre,
    order_ids,
    fetch_list,
    scan_tiles,
    block_tile,
    block_pix,
    noise_kernel,
    scan_weight,
):
    highest = lax.Precision.HIGHEST
    device_count = lax.axis_size("dev")
    position = lax.axis_index("dev")
    both_halves = lax.all_gather(alm, "half", axis=2, tiled=True)
    mixed_alm = jnp.einsum(
        "fg,scgl->scfl", field_mix, both_halves.astype(jnp.float32), precision=highest
    ).astype(jnp.bfloat16)
    cycle_coeff = jnp.einsum(
        "scfl,slr->rscf", mixed_alm, legendre, preferred_element_type=jnp.float32
    ).astype(jnp.bfloat16)
    by_cycle = lax.all_to_all(cycle_coeff, "dev", split_axis=0, concat_axis=1, tiled=True)
    cycle_count = by_cycle.shape[0]
    order_count = by_cycle.shape[1]
    field_count = by_cycle.shape[3]
    pixel_block = 512
    block_count = NPHI // pixel_block
    weights = jnp.where(order_ids == 0, 1.0, 2.0).astype(jnp.float32) / math.sqrt(2.0 * order_count)

    def cycle_block(start):
        pixel_iota = start + jnp.arange(pixel_block, dtype=jnp.int32)
        phase_steps = order_ids[:, None] * (2 * pixel_iota[None, :] + 1) % (2 * NPHI)
        angles = phase_steps.astype(jnp.float32) * (math.pi / NPHI)
        fourier = jnp.stack(
            [weights[:, None] * jnp.cos(angles), -weights[:, None] * jnp.sin(angles)], axis=1
        ).astype(jnp.bfloat16)
        return jnp.einsum(
            "rscf,scj->rfj", by_cycle, fourier, preferred_element_type=jnp.float32
        ).astype(jnp.bfloat16)

    starts = jnp.arange(block_count, dtype=jnp.int32) * pixel_block
    cycle_blocks = lax.map(cycle_block, starts)
    per_block = pixel_block // TILE
    map_tiles = cycle_blocks.reshape(block_count, cycle_count, field_count, per_block, TILE)
    map_tiles = map_tiles.transpose(1, 0, 3, 2, 4).reshape(
        cycle_count * block_count * per_block, field_count, TILE
    )
    tile_count = map_tiles.shape[0]
    slot_capacity = fetch_list.shape[2]
    owner_row = lax.dynamic_index_in_dim(fetch_list, position, 0, keepdims=False)
    every_tile = lax.all_gather(map_tiles, "dev", axis=0, tiled=True)
    my_column = lax.dynamic_index_in_dim(fetch_list, position, 1, keepdims=False)
    global_ids = jnp.arange(device_count, dtype=jnp.int32)[:, None] * tile_count + jnp.maximum(
        my_column, 0
    )
    fetched = every_tile[global_ids] * (my_column >= 0).astype(jnp.bfloat16)[:, :, None, None]
    slot_total = device_count * slot_capacity
    flat_fetched = fetched.reshape(slot_total, field_count, TILE)
    scan_count = block_tile.shape[0]
    block_total = block_tile.shape[1]
    slot_index = jnp.take_along_axis(scan_tiles, block_tile, axis=1)
    block_tiles = flat_fetched[slot_index]
    pixels = block_pix.reshape(scan_count, block_total, BLK)
    one_hot = (
        pixels[:, :, None, :] == jnp.arange(TILE, dtype=jnp.int32)[None, None, :, None]
    ).astype(jnp.bfloat16)
    samples = jnp.einsum(
        "sbfp,sbpt->sbft", block_tiles, one_hot, preferred_element_type=jnp.float32
    ).astype(jnp.bfloat16)
    taps = noise_kernel.astype(jnp.bfloat16)
    near_band = jnp.concatenate([taps[:, ::-1], taps[:, 1:]], axis=1)
    far_band = jnp.concatenate(
        [jnp.zeros((scan_count, BLK), jnp.bfloat16), taps[:, 1:][:, ::-1]], axis=1
    )
    near_table = toeplitz_rows(near_band, BLK)
    far_table = toeplitz_rows(far_band, BLK)
    earlier = jnp.pad(samples[:, :-1], ((0, 0), (1, 0), (0, 0), (0, 0)))
    later = jnp.pad(samples[:, 1:], ((0, 0), (0, 1), (0, 0), (0, 0)))
    filtered = jnp.einsum("sbfu,stu->sbft", samples, near_table, preferred_element_type=jnp.float32)
    filtered = filtered + jnp.einsum(
        "sbfu,stu->sbft", earlier, far_table, preferred_element_type=jnp.float32
    )
    filtered = filtered + jnp.einsum(
        "sbfu,sut->sbft", later, far_table, preferred_element_type=jnp.float32
    )
    weighted = (scan_weight[:, None, None, None] * filtered).astype(jnp.bfloat16)
    partial_value = jnp.einsum(
        "sbft,sbpt->sbfp", weighted, one_hot, preferred_element_type=jnp.float32
    )
    flat_slots = slot_index.reshape(-1)
    slot_select = (jnp.arange(slot_total, dtype=jnp.int32)[:, None] == flat_slots[None, :]).astype(
        jnp.float32
    )
    per_slot = jnp.dot(
        slot_select,
        partial_value.reshape(scan_count * block_total, field_count * TILE),
        precision=highest,
    )
    per_slot = per_slot.reshape(device_count, slot_capacity, field_count, TILE)
    returned = lax.all_to_all(per_slot, "dev", split_axis=0, concat_axis=0, tiled=True)
    owner_select = (
        jnp.arange(tile_count, dtype=jnp.int32)[:, None] == owner_row.reshape(-1)[None, :]
    ).astype(jnp.float32)
    own_tiles = jnp.dot(
        owner_select, returned.reshape(slot_total, field_count * TILE), precision=highest
    )
    binned = own_tiles.reshape(cycle_count, NPHI // TILE, field_count, TILE).transpose(0, 2, 1, 3)
    return binned.reshape(cycle_count, field_count, NPHI)


def solution(mesh):
    return jax.shard_map(
        local,
        mesh=mesh,
        in_specs=(
            P("half", None),
            P("dev", None, "half", None),
            P("dev", None, None),
            P(),
            P(),
            P("dev", None),
            P("dev", None),
            P("dev", None),
            P("dev", None),
            P("dev"),
        ),
        out_specs=P("dev", "half", None),
        check_vma=False,
    )
```

profile of v0, /device:TPU:32, one launch (start us, length us, event | category | flops | bytes accessed | tf_op | source)
XLA Modules:
  0.0 397.3 jit_solution(6174108100497894636)
XLA Ops:
  6.5 0.7 all-gather.3.cloned.1.call-update
  7.3 20.4 %all-gather.3.cloned.1.call-done = bf16[8,2,32,2048]{3,2,1,0:T(8,128)(2,1)} async-done(((bf16[8,2,16,2048]{3,2,1,0:T(8,128)(2,1)}), bf16[8,2,32,2048]{3,2,1,0:T(8,128)(2,1)}) %all-gather.3.cloned.1.call-update) | async-done | bytes 2097168 | tf_op jit(solution)/shard_map/all_gather | solution.py:38
  27.7 2.8 fusion.27
  30.5 3.0 fusion.36
  33.4 0.5 copy.40
  33.9 1.0 reshape.451
  34.9 13.7 %all-to-all-start = ((bf16[128,2,128]{2,1,0:T(2,128)(2,1)}), bf16[128,2,128]{2,1,0:T(2,128)(2,1)S(1)}, u32[]{:S(2)}, u32[]{:S(2)}) async-start(bf16[128,2,128]{2,1,0:T(2,128)(2,1)} %reshape.451), calls=%async_computation | async-start | bytes 131072 | tf_op jit(solution)/shard_map/all_to_all | solution.py:45
  48.8 10.8 %all-to-all-done = bf16[128,2,128]{2,1,0:T(2,128)(2,1)S(1)} async-done(((bf16[128,2,128]{2,1,0:T(2,128)(2,1)}), bf16[128,2,128]{2,1,0:T(2,128)(2,1)S(1)}, u32[]{:S(2)}, u32[]{:S(2)}) %all-to-all-start) | async-done | bytes 65568 | tf_op jit(solution)/shard_map/all_to_all | solution.py:45
  60.4 88.3 %while.12 = (s32[]{:T(128)}, bf16[8,1,16,512]{3,2,1,0:T(8,128)(2,1)S(1)}, f32[1024]{0:T(1024)S(1)}, s32[1024]{0:T(1024)S(1)}, s32[8]{0:T(128)S(1)}, /*index=5*/f...) while((s32[]{:T(128)}, bf16[8,1,16,512]{3,2,1,0:T(8,128)(2,1)S(1)}, f32[1024]{0:T(1024)S(1)}, ...), condition=%wide.region_1.2_spmd, body=%wide.region_0.1_spmd.sunk | while | flops 44049920 | bytes 4292721 | solution.py:65
  60.4 0.6 dynamic_slice.20
  61.0 0.6 multiply_add_fusion.3
  61.6 9.4 %multiply_convert_fusion.4 = (bf16[1024,1,512]{2,0,1:T(8,128)(2,1)S(1)}, bf16[1024,1,512]{2,0,1:T(8,128)(2,1)S(1)}) fusion(s32[512]{0:T(512)S(1)} %multiply_add_fusion.3, s32[1024]{0:T(1024)S(1)} %get-tuple-element.204, f32[1024]{0:T(1024)S(1)} %get-tuple-element.203, f32[1024]{0:T(1024)S(1)} %bitcast.147), kind=kLoop, calls=%fused_computation.16.clone.1 | loop fusion | flops 9437184 | bytes 2111488 | tf_op jit(solution)/shard_map/convert
  71.0 0.4 fusion.64
  71.4 0.6 dynamic_slice.20
  72.0 0.6 multiply_add_fusion.3
  72.7 9.4 %multiply_convert_fusion.4 = (bf16[1024,1,512]{2,0,1:T(8,128)(2,1)S(1)}, bf16[1024,1,512]{2,0,1:T(8,128)(2,1)S(1)}) fusion(s32[512]{0:T(512)S(1)} %multiply_add_fusion.3, s32[1024]{0:T(1024)S(1)} %get-tuple-element.204, f32[1024]{0:T(1024)S(1)} %get-tuple-element.203, f32[1024]{0:T(1024)S(1)} %bitcast.147), kind=kLoop, calls=%fused_computation.16.clone.1 | loop fusion | flops 9437184 | bytes 2111488 | tf_op jit(solution)/shard_map/convert
  82.5 0.6 dynamic_slice.20
  83.1 0.6 multiply_add_fusion.3
  83.7 9.4 %multiply_convert_fusion.4 = (bf16[1024,1,512]{2,0,1:T(8,128)(2,1)S(1)}, bf16[1024,1,512]{2,0,1:T(8,128)(2,1)S(1)}) fusion(s32[512]{0:T(512)S(1)} %multiply_add_fusion.3, s32[1024]{0:T(1024)S(1)} %get-tuple-element.204, f32[1024]{0:T(1024)S(1)} %get-tuple-element.203, f32[1024]{0:T(1024)S(1)} %bitcast.147), kind=kLoop, calls=%fused_computation.16.clone.1 | loop fusion | flops 9437184 | bytes 2111488 | tf_op jit(solution)/shard_map/convert
  93.5 0.6 dynamic_slice.20
  94.1 0.6 multiply_add_fusion.3
  94.8 9.4 %multiply_convert_fusion.4 = (bf16[1024,1,512]{2,0,1:T(8,128)(2,1)S(1)}, bf16[1024,1,512]{2,0,1:T(8,128)(2,1)S(1)}) fusion(s32[512]{0:T(512)S(1)} %multiply_add_fusion.3, s32[1024]{0:T(1024)S(1)} %get-tuple-element.204, f32[1024]{0:T(1024)S(1)} %get-tuple-element.203, f32[1024]{0:T(1024)S(1)} %bitcast.147), kind=kLoop, calls=%fused_computation.16.clone.1 | loop fusion | flops 9437184 | bytes 2111488 | tf_op jit(solution)/shard_map/convert
  104.6 0.6 dynamic_slice.20
  105.1 0.6 multiply_add_fusion.3
  105.8 9.4 %multiply_convert_fusion.4 = (bf16[1024,1,512]{2,0,1:T(8,128)(2,1)S(1)}, bf16[1024,1,512]{2,0,1:T(8,128)(2,1)S(1)}) fusion(s32[512]{0:T(512)S(1)} %multiply_add_fusion.3, s32[1024]{0:T(1024)S(1)} %get-tuple-element.204, f32[1024]{0:T(1024)S(1)} %get-tuple-element.203, f32[1024]{0:T(1024)S(1)} %bitcast.147), kind=kLoop, calls=%fused_computation.16.clone.1 | loop fusion | flops 9437184 | bytes 2111488 | tf_op jit(solution)/shard_map/convert
  115.6 0.6 dynamic_slice.20
  116.2 0.6 multiply_add_fusion.3
  116.8 9.4 %multiply_convert_fusion.4 = (bf16[1024,1,512]{2,0,1:T(8,128)(2,1)S(1)}, bf16[1024,1,512]{2,0,1:T(8,128)(2,1)S(1)}) fusion(s32[512]{0:T(512)S(1)} %multiply_add_fusion.3, s32[1024]{0:T(1024)S(1)} %get-tuple-element.204, f32[1024]{0:T(1024)S(1)} %get-tuple-element.203, f32[1024]{0:T(1024)S(1)} %bitcast.147), kind=kLoop, calls=%fused_computation.16.clone.1 | loop fusion | flops 9437184 | bytes 2111488 | tf_op jit(solution)/shard_map/convert
  126.6 0.6 dynamic_slice.20
  127.2 0.6 multiply_add_fusion.3
  127.9 9.4 %multiply_convert_fusion.4 = (bf16[1024,1,512]{2,0,1:T(8,128)(2,1)S(1)}, bf16[1024,1,512]{2,0,1:T(8,128)(2,1)S(1)}) fusion(s32[512]{0:T(512)S(1)} %multiply_add_fusion.3, s32[1024]{0:T(1024)S(1)} %get-tuple-element.204, f32[1024]{0:T(1024)S(1)} %get-tuple-element.203, f32[1024]{0:T(1024)S(1)} %bitcast.147), kind=kLoop, calls=%fused_computation.16.clone.1 | loop fusion | flops 9437184 | bytes 2111488 | tf_op jit(solution)/shard_map/convert
  137.7 0.6 dynamic_slice.20
  138.3 0.6 multiply_add_fusion.3
  138.9 9.4 %multiply_convert_fusion.4 = (bf16[1024,1,512]{2,0,1:T(8,128)(2,1)S(1)}, bf16[1024,1,512]{2,0,1:T(8,128)(2,1)S(1)}) fusion(s32[512]{0:T(512)S(1)} %multiply_add_fusion.3, s32[1024]{0:T(1024)S(1)} %get-tuple-element.204, f32[1024]{0:T(1024)S(1)} %get-tuple-element.203, f32[1024]{0:T(1024)S(1)} %bitcast.147), kind=kLoop, calls=%fused_computation.16.clone.1 | loop fusion | flops 9437184 | bytes 2111488 | tf_op jit(solution)/shard_map/convert
  148.8 0.7 copy.43
  150.9 1.5 gather_fusion.2
  152.8 0.5 broadcast_bitcast_fusion.1
  153.3 3.2 copy.59
  156.5 3.1 slice.36
  159.6 5.8 %reshape.447 = bf16[2095104]{0:T(1024)(128)(2,1)} reshape(bf16[4,523776]{1,0:T(4,128)(2,1)} %slice.36) | data formatting | bytes 8380416
  165.4 10.1 %reshape.402 = bf16[4,512,1023]{2,1,0:T(8,128)(2,1)} reshape(bf16[2095104]{0:T(1024)(128)(2,1)} %reshape.447) | data formatting | bytes 8380416 | tf_op jit(solution)/shard_map/reshape | solution.py:17
  175.4 0.7 reverse
  176.3 0.5 broadcast_bitcast_fusion
  176.8 3.2 copy.60
  180.1 3.2 slice.39
  183.2 5.7 %reshape.449 = bf16[2095104]{0:T(1024)(128)(2,1)} reshape(bf16[4,523776]{1,0:T(4,128)(2,1)} %slice.39) | data formatting | bytes 8380416
  189.0 10.1 %reshape.403 = bf16[4,512,1023]{2,1,0:T(8,128)(2,1)} reshape(bf16[2095104]{0:T(1024)(128)(2,1)} %reshape.449) | data formatting | bytes 8380416 | tf_op jit(solution)/shard_map/reshape | solution.py:17
  199.2 92.8 %all-gather.5.cloned.1.call-done = bf16[4096,16,128]{2,1,0:T(8,128)(2,1)} async-done(((bf16[32,16,128]{2,1,0:T(8,128)(2,1)}), bf16[4096,16,128]{2,1,0:T(8,128)(2,1)}) %all-gather.5.cloned.1.call-update) | async-done | bytes 16777232 | tf_op jit(solution)/shard_map/all_gather | solution.py:74
  292.0 6.6 %gather_fusion = bf16[256,16,128]{2,1,0:T(8,128)(2,1)S(1)} fusion(bf16[4096,16,128]{2,1,0:T(8,128)(2,1)} %all-gather.5.cloned.1.call-done, s32[1024]{0:T(1024)S(1)} %pad_clamp_fusion.1), kind=kCustom, calls=%fused_computation | custom fusion | bytes 2098176 | tf_op jit(solution)/shard_map/gather | solution.py:79
  298.9 0.7 gather_fusion.1
  299.6 5.3 %fusion.32 = bf16[4,32,16,512]{3,2,1,0:T(8,128)(2,1)S(1)} fusion(bf16[4,32,16,128]{3,2,1,0:T(8,128)(2,1)S(1)} %bitcast.140, s32[4,32,512]{2,1,0:T(8,128)S(1)} %bitcast.144), kind=kOutput, calls=%fused_computation.43 | convolution fusion | flops 277872640 | bytes 2883584 | tf_op jit(solution)/shard_map/sbfp,sbpt->sbft/dot_general | solution.py:90
  305.0 1.4 fusion.28
  306.4 0.8 copy-done.2
  307.2 1.4 fusion.30
  308.6 1.7 multiply_convert_fusion.2
  310.3 5.0 %fusion.21 = f32[4,32,16,128]{3,2,1,0:T(8,128)S(1)} fusion(bf16[4,32,16,512]{3,2,1,0:T(8,128)(2,1)S(1)} %multiply_convert_fusion.2, s32[4,32,512]{2,1,0:T(8,128)S(1)} %bitcast.145), kind=kOutput, calls=%fused_computation.25 | convolution fusion | flops 276824064 | bytes 3407872 | tf_op jit(solution)/shard_map/sbft,sbpt->sbfp/dot_general | solution.py:110
  316.0 1.0 fusion.39
  317.0 2.5 copy.48
  319.6 11.5 %all-to-all-start.1 = ((f32[128,2,16,128]{3,2,1,0:T(8,128)}), f32[128,2,16,128]{3,2,1,0:T(8,128)S(1)}, u32[]{:S(2)}, u32[]{:S(2)}) async-start(f32[128,2,16,128]{3,2,1,0:T(8,128)} %copy.48), calls=%async_computation.1 | async-start | bytes 4194304 | tf_op jit(solution)/shard_map/all_to_all | solution.py:123
  331.3 52.8 %all-to-all-done.1 = f32[128,2,16,128]{3,2,1,0:T(8,128)S(1)} async-done(((f32[128,2,16,128]{3,2,1,0:T(8,128)}), f32[128,2,16,128]{3,2,1,0:T(8,128)S(1)}, u32[]{:S(2)}, u32[]{:S(2)}) %all-to-all-start.1) | async-done | bytes 2097184 | tf_op jit(solution)/shard_map/all_to_all | solution.py:123
  384.2 2.2 copy.66
  386.4 1.9 copy.49
  388.3 1.1 convolution_bitcast_fusion
  389.4 0.8 reshape.406
  (64 shorter events, 6.8 us)
Async XLA Ops:
  6.5 143.4 %copy-start = (s32[128,128,2]{1,2,0:T(2,128)S(1)}, s32[128,128,2]{1,2,0:T(2,128)}, u32[]{:S(2)}) copy-start(s32[128,128,2]{1,2,0:T(2,128)} %param.16) | copy-start | bytes 393220
  6.5 21.1 %all-gather.3.cloned.1.call-start = ((), (), s32[]{:S(2)}) async-start(), calls=%async_computation.2 | async-start | bytes 3145728 | tf_op jit(solution)/shard_map/all_gather | solution.py:38
  30.4 18.3 %copy-start.5 = (s32[1024]{0:T(1024)S(1)}, s32[1024]{0:T(1024)}, u32[]{:S(2)}) copy-start(s32[1024]{0:T(1024)} %param.15) | copy-start | bytes 12292
  34.9 24.8 %all-to-all-start = ((bf16[128,2,128]{2,1,0:T(2,128)(2,1)}), bf16[128,2,128]{2,1,0:T(2,128)(2,1)S(1)}, u32[]{:S(2)}, u32[]{:S(2)}) async-start(bf16[128,2,128]{2,1,0:T(2,128)(2,1)} %reshape.451), calls=%async_computation | async-start | bytes 131072 | tf_op jit(solution)/shard_map/all_to_all | solution.py:45
  48.6 243.4 %all-gather.5.cloned.1.call-start = ((), (), s32[]{:S(2)}) async-start(), calls=%async_computation.3 | async-start | bytes 16908288 | tf_op jit(solution)/shard_map/all_gather | solution.py:74
  60.4 89.1 %copy-start.6 = (f32[4,512]{1,0:T(4,128)S(1)}, f32[4,512]{1,0:T(4,128)}, u32[]{:S(2)}) copy-start(f32[4,512]{1,0:T(4,128)} %param.20) | copy-start | bytes 24580
  60.4 90.5 %copy-start.7 = (s32[4,32]{1,0:T(4,128)S(1)}, s32[4,32]{1,0:T(4,128)}, u32[]{:S(2)}) copy-start(s32[4,32]{1,0:T(4,128)} %param.18) | copy-start | bytes 1540
  148.7 2.2 copy-start.1
  148.7 3.9 copy-start.4
  299.6 5.4 %copy-start.3 = (bf16[4,512,1023]{2,1,0:T(8,128)(2,1)S(1)}, bf16[4,512,1023]{2,1,0:T(8,128)(2,1)}, u32[]{:S(2)}) copy-start(bf16[4,512,1023]{2,1,0:T(8,128)(2,1)} %reshape.402) | copy-start | bytes 12570628
  305.0 2.2 copy-start.2
  307.2 1.4 copy-start.8
  319.6 64.6 %all-to-all-start.1 = ((f32[128,2,16,128]{3,2,1,0:T(8,128)}), f32[128,2,16,128]{3,2,1,0:T(8,128)S(1)}, u32[]{:S(2)}, u32[]{:S(2)}) async-start(f32[128,2,16,128]{3,2,1,0:T(8,128)} %copy.48), calls=%async_computation.1 | async-start | bytes 4194304 | tf_op jit(solution)/shard_map/all_to_all | solution.py:123
Sparse Core Ops, SparseCore 0:
  9.1 18.5 all-gather.2
  149.6 142.3 all-gather.4
where the time goes:
time: 401 us; the launch traced here: 397 us
  waiting for transfers between devices  178 us (44%)
  other arithmetic  80.8 us (20%)
  local copies, waits for them, and re-layouts  73.5 us (18%)
  matrix products  25.8 us (6%)
  starting transfers between devices  25.4 us (6%)
  between operations  14 us (3%)
    all_gather x1, waiting for transfers between devices, local(): every_tile = lax.all_gather(map_tiles, 'dev', axis=0, tiled=True)  92.8 us
    another operation x8, other arithmetic  75.2 us
    all_to_all x1, waiting for transfers between devices, local(): lax.all_to_all(per_slot, 'dev', split_axis=0, concat_axis=0, tiled=True)  52.8 us
    unnamed x32, local copies, waits for them, and re-layouts  24.7 us
    all_gather x1, waiting for transfers between devices, local(): both_halves = lax.all_gather(alm, 'half', axis=2, tiled=True)  20.4 us
    reshape x2, local copies, waits for them, and re-layouts, toeplitz_rows(): repeated[:, :block_len * (2 * block_len - 1)]  20.2 us
    all_to_all x1, starting transfers between devices, local(): lax.all_to_all(cycle_coeff, 'dev', split_axis=0, concat_axis=1, tiled=True)  13.7 us
    all_to_all x1, starting transfers between devices, local(): lax.all_to_all(per_slot, 'dev', split_axis=0, concat_axis=0, tiled=True)  11.5 us
  transfers between devices with their start and end apart: 4, of which 4 were waited for; matrix products, arithmetic and copies ran while one was open for 13% of the time, Pallas kernels for 0%

commit v1 on v0

v1 whole, which is shorter than its diff:
```python
import math

import jax
import jax.numpy as jnp
from jax import lax
from jax.experimental import pallas as pl
from jax.experimental.pallas import tpu as pltpu
from jax.sharding import PartitionSpec as P

NPHI = 4096
TILE = 128
BLK = 512
HALF_BLK = 256
F32 = jnp.float32
BF16 = jnp.bfloat16
VMEM_LIMIT = 60 * 1024 * 1024


def legendre_kernel(alm_hbm, leg_hbm, out_ref, alm_buf, leg_buf, sems):
    orders = leg_buf.shape[0]
    copies = []
    for s in range(orders):
        a = pltpu.make_async_copy(alm_hbm.at[s], alm_buf.at[s], sems.at[0, s])
        b = pltpu.make_async_copy(leg_hbm.at[s], leg_buf.at[s], sems.at[1, s])
        a.start()
        b.start()
        copies.append((a, b))
    for s in range(orders):
        copies[s][0].wait()
        copies[s][1].wait()
        rows = alm_buf.shape[1]
        out_ref[pl.ds(s * rows, rows), :] = jnp.dot(
            alm_buf[s], leg_buf[s], preferred_element_type=F32
        )


def contract_ells(alm, legendre):
    orders, parts, fields, ells = alm.shape
    cycles = legendre.shape[2]
    rows = parts * fields
    return pl.pallas_call(
        legendre_kernel,
        out_shape=jax.ShapeDtypeStruct((orders * rows, cycles), F32),
        in_specs=[pl.BlockSpec(memory_space=pl.ANY), pl.BlockSpec(memory_space=pl.ANY)],
        scratch_shapes=[
            pltpu.VMEM((orders, rows, ells), BF16),
            pltpu.VMEM((orders, ells, cycles), BF16),
            pltpu.SemaphoreType.DMA((2, orders)),
        ],
        compiler_params=pltpu.CompilerParams(vmem_limit_bytes=VMEM_LIMIT),
        name="contract_ells",
    )(alm.reshape(orders, rows, ells), legendre)


def mix_kernel(own_ref, other_ref, mix_ref, out_ref):
    fields = mix_ref.shape[1]
    rows = own_ref.shape[0]
    highest = lax.Precision.HIGHEST
    row_group = lax.broadcasted_iota(jnp.int32, (rows, rows), 0) // fields
    col_group = lax.broadcasted_iota(jnp.int32, (rows, rows), 1) // fields
    spread = (
        lax.broadcasted_iota(jnp.int32, (rows, fields), 0) % fields
        == lax.broadcasted_iota(jnp.int32, (rows, fields), 1)
    ).astype(F32)
    spread_t = (
        lax.broadcasted_iota(jnp.int32, (fields, rows), 1) % fields
        == lax.broadcasted_iota(jnp.int32, (fields, rows), 0)
    ).astype(F32)

    def mixed(mix, values):
        wide = jnp.dot(
            jnp.dot(spread, mix, precision=highest, preferred_element_type=F32),
            spread_t,
            precision=highest,
            preferred_element_type=F32,
        )
        wide = jnp.where(row_group == col_group, wide, 0.0)
        return jnp.dot(wide, values, precision=highest, preferred_element_type=F32)

    total = mixed(mix_ref[0], own_ref[...]) + mixed(mix_ref[1], other_ref[...])
    by_cycle = total.T.astype(BF16)
    lanes = out_ref.shape[2]
    for p in range(out_ref.shape[1]):
        out_ref[:, p, :] = by_cycle[:, p * lanes : (p + 1) * lanes]


def mix_fields(own, other, mix_pair):
    rows, cycles = own.shape
    return pl.pallas_call(
        mix_kernel,
        out_shape=jax.ShapeDtypeStruct((cycles, rows // 128, 128), BF16),
        compiler_params=pltpu.CompilerParams(vmem_limit_bytes=VMEM_LIMIT),
        name="mix_fields",
    )(own, other, mix_pair)


def synth_kernel(owner_ref, coeff_ref, turn_ref, table_ref, out_ref, lhs_ref, map_ref):
    devices, groups, lanes = coeff_ref.shape
    tiles, fields = map_ref.shape[0], map_ref.shape[1]
    slots = turn_ref.shape[2]
    per_group = slots // groups
    k_half = slots * devices
    flipped = [coeff_ref[:, g, :].astype(F32).T for g in range(groups)]
    for s in range(slots):
        block = flipped[s // per_group]
        at = (s % per_group) * 2 * fields
        real = block[at : at + fields]
        imag = block[at + fields : at + 2 * fields]
        for j in range(tiles):
            cos_row = turn_ref[0, j, s : s + 1, :]
            sin_row = turn_ref[1, j, s : s + 1, :]
            rows = pl.ds(j * fields, fields)
            lhs_ref[rows, pl.ds(s * devices, devices)] = (real * cos_row - imag * sin_row).astype(
                BF16
            )
            lhs_ref[rows, pl.ds(k_half + s * devices, devices)] = (
                real * sin_row + imag * cos_row
            ).astype(BF16)
    pixels = jnp.dot(lhs_ref[...], table_ref[...], preferred_element_type=F32).astype(BF16)
    map_ref[...] = pixels.reshape(tiles, fields, TILE)
    capacity = out_ref.shape[1]

    def pick(e, carry):
        for k in range(capacity):
            g = jnp.maximum(owner_ref[k, e], 0)
            out_ref[e, k] = map_ref[g]
        return carry

    lax.fori_loop(0, out_ref.shape[0], pick, 0, unroll=8)


def synthesize(owner_row, coeff, turns, table, fields):
    capacity, devices = owner_row.shape
    tiles = turns.shape[1]
    k_total = table.shape[0]
    return pl.pallas_call(
        synth_kernel,
        out_shape=jax.ShapeDtypeStruct((devices, capacity, fields, TILE), BF16),
        in_specs=[
            pl.BlockSpec(memory_space=pltpu.SMEM),
            pl.BlockSpec(memory_space=pltpu.VMEM),
            pl.BlockSpec(memory_space=pltpu.VMEM),
            pl.BlockSpec(memory_space=pltpu.VMEM),
        ],
        scratch_shapes=[
            pltpu.VMEM((tiles * fields, k_total), BF16),
            pltpu.VMEM((tiles, fields, TILE), BF16),
        ],
        compiler_params=pltpu.CompilerParams(vmem_limit_bytes=VMEM_LIMIT),
        name="synthesize",
    )(owner_row, coeff, turns, table)


def band_kernel(row_ref, out_ref):
    rows, width = out_ref.shape[1], out_ref.shape[2]
    wide = jnp.broadcast_to(row_ref[0], (rows, width))
    out_ref[0] = pltpu.roll(wide, 0, 1, stride=1, stride_axis=0).astype(BF16)


def band_strips(rows):
    scans, _, width = rows.shape
    return pl.pallas_call(
        band_kernel,
        grid=(scans,),
        out_shape=jax.ShapeDtypeStruct((scans, HALF_BLK, width), BF16),
        in_specs=[pl.BlockSpec((1, 1, width), lambda n: (n, 0, 0))],
        out_specs=pl.BlockSpec((1, HALF_BLK, width), lambda n: (n, 0, 0)),
        compiler_params=pltpu.CompilerParams(vmem_limit_bytes=VMEM_LIMIT),
        name="band_strips",
    )(rows)


def scan_kernel(
    list_ref, entry_ref, weight_ref, tiles_ref, pix_ref, strip_ref, out_ref, pad_ref, wtd_ref, sum_ref
):
    n = pl.program_id(0)
    fields = tiles_ref.shape[1]
    blocks = entry_ref.shape[1]
    halves = 2 * blocks
    edge = 2 * fields

    @pl.when(n == 0)
    def _():
        sum_ref[...] = jnp.zeros_like(sum_ref)
        pad_ref[pl.ds(0, edge), :] = jnp.zeros((edge, HALF_BLK), BF16)
        pad_ref[pl.ds(edge + halves * fields, edge), :] = jnp.zeros((edge, HALF_BLK), BF16)

    per_half = HALF_BLK // TILE
    quarters = BLK // TILE

    def gather(b, carry):
        slot = list_ref[n, entry_ref[n, b]]
        tile = tiles_ref[slot].astype(F32)
        for q in range(quarters):
            row = pix_ref[0, pl.ds(b * quarters + q, 1), :]
            at = jnp.broadcast_to(row, (8, TILE))
            live = at >= 0
            index = jnp.maximum(at, 0)
            parts = [
                jnp.where(
                    live,
                    jnp.take_along_axis(
                        tile[8 * i : 8 * i + 8], index, axis=1, mode="promise_in_bounds"
                    ),
                    0.0,
                )
                for i in range(fields // 8)
            ]
            start = pl.multiple_of(edge + (2 * b + q // per_half) * fields, fields)
            pad_ref[pl.ds(start, fields), pl.ds((q % per_half) * TILE, TILE)] = jnp.concatenate(
                parts, axis=0
            ).astype(BF16)
        return carry

    lax.fori_loop(0, blocks, gather, 0, unroll=4)
    total = None
    for d in range(-2, 3):
        term = jnp.dot(
            pad_ref[pl.ds(edge - d * fields, halves * fields), :],
            strip_ref[0, :, pl.ds((d + 2) * HALF_BLK, HALF_BLK)],
            preferred_element_type=F32,
        )
        total = term if total is None else total + term
    wtd_ref[...] = (weight_ref[n] * total).astype(BF16)
    pixel_iota = lax.broadcasted_iota(jnp.int32, (TILE, TILE), 0)

    def bin_block(b, carry):
        slot = list_ref[n, entry_ref[n, b]]
        partial = None
        for q in range(quarters):
            row = pix_ref[0, pl.ds(b * quarters + q, 1), :]
            hot = (pixel_iota == row).astype(F32).astype(BF16)
            start = pl.multiple_of((2 * b + q // per_half) * fields, fields)
            values = wtd_ref[pl.ds(start, fields), pl.ds((q % per_half) * TILE, TILE)]
            term = lax.dot_general(
                values, hot, (((1,), (1,)), ((), ())), preferred_element_type=F32
            )
            partial = term if partial is None else partial + term
        sum_ref[slot] = sum_ref[slot] + partial
        return carry

    lax.fori_loop(0, blocks, bin_block, 0, unroll=4)

    @pl.when(n == pl.num_programs(0) - 1)
    def _():
        out_ref[...] = sum_ref[...].astype(BF16)


def scan_stage(scan_tiles, block_tile, scan_weight, tiles, pix, strips):
    slots, fields, _ = tiles.shape
    scans, blocks = block_tile.shape
    rows = blocks * BLK // TILE
    width = strips.shape[2]
    smem = pl.BlockSpec(memory_space=pltpu.SMEM)
    whole = pl.BlockSpec((slots, fields, TILE), lambda n: (0, 0, 0))
    return pl.pallas_call(
        scan_kernel,
        grid=(scans,),
        out_shape=jax.ShapeDtypeStruct((slots, fields, TILE), BF16),
        in_specs=[
            smem,
            smem,
            smem,
            whole,
            pl.BlockSpec((1, rows, TILE), lambda n: (n, 0, 0)),
            pl.BlockSpec((1, HALF_BLK, width), lambda n: (n, 0, 0)),
        ],
        out_specs=whole,
        scratch_shapes=[
            pltpu.VMEM(((2 * blocks + 4) * fields, HALF_BLK), BF16),
            pltpu.VMEM((2 * blocks * fields, HALF_BLK), BF16),
            pltpu.VMEM((slots, fields, TILE), F32),
        ],
        compiler_params=pltpu.CompilerParams(
            vmem_limit_bytes=VMEM_LIMIT, dimension_semantics=("arbitrary",)
        ),
        name="scan_stage",
    )(scan_tiles, block_tile, scan_weight, tiles, pix, strips)


def owner_kernel(owner_ref, back_ref, out_ref, sum_ref):
    capacity, devices = owner_ref.shape
    tiles = sum_ref.shape[1] - 1
    sum_ref[...] = jnp.zeros_like(sum_ref)

    def add(e, carry):
        for k in range(capacity):
            g = owner_ref[k, e]
            g = jnp.where(g < 0, tiles, g)
            sum_ref[k, g] = sum_ref[k, g] + back_ref[e, k].astype(F32)
        return carry

    lax.fori_loop(0, devices, add, 0, unroll=8)
    for g in range(tiles):
        total = sum_ref[0, g]
        for k in range(1, capacity):
            total = total + sum_ref[k, g]
        out_ref[0, :, pl.ds(g * TILE, TILE)] = total


def owner_sum(owner_row, returned):
    devices, capacity, fields, _ = returned.shape
    tiles = NPHI // TILE
    return pl.pallas_call(
        owner_kernel,
        out_shape=jax.ShapeDtypeStruct((1, fields, NPHI), F32),
        in_specs=[pl.BlockSpec(memory_space=pltpu.SMEM), pl.BlockSpec(memory_space=pltpu.VMEM)],
        scratch_shapes=[pltpu.VMEM((capacity, tiles + 1, fields, TILE), F32)],
        compiler_params=pltpu.CompilerParams(vmem_limit_bytes=VMEM_LIMIT),
        name="owner_sum",
    )(owner_row, returned)


def local(
    field_mix,
    alm,
    legendre,
    order_ids,
    fetch_list,
    scan_tiles,
    block_tile,
    block_pix,
    noise_kernel,
    scan_weight,
):
    half = lax.axis_index("half")
    position = lax.axis_index("dev")
    devices = fetch_list.shape[0]
    fields = alm.shape[2]
    slots = alm.shape[0]
    order_count = order_ids.shape[0]
    scans = block_pix.shape[0]
    tile_count = NPHI // TILE

    own = contract_ells(alm, legendre)
    other = lax.ppermute(own, "half", [(0, 1), (1, 0)])
    low, high = field_mix[:, :fields], field_mix[:, fields:]
    mix_pair = jnp.stack(
        [jnp.where(half == 0, low, high), jnp.where(half == 0, high, low)], axis=0
    )
    sent = mix_fields(own, other, mix_pair)
    coeff = lax.all_to_all(sent, "dev", split_axis=0, concat_axis=0, tiled=True)

    ids = order_ids.reshape(devices, slots).T
    tile_iota = jnp.arange(tile_count, dtype=jnp.int32)
    turn_angle = ((ids[None] * tile_iota[:, None, None]) % tile_count).astype(F32) * (
        2.0 * math.pi / tile_count
    )
    turns = jnp.stack([jnp.cos(turn_angle), jnp.sin(turn_angle)], axis=0)
    flat_ids = ids.reshape(-1)
    pixel_iota = jnp.arange(TILE, dtype=jnp.int32)
    steps = flat_ids[:, None] * (2 * pixel_iota[None, :] + 1) % (2 * NPHI)
    angles = steps.astype(F32) * (math.pi / NPHI)
    weights = jnp.where(flat_ids == 0, 1.0, 2.0).astype(F32) / math.sqrt(2.0 * order_count)
    table = jnp.concatenate(
        [weights[:, None] * jnp.cos(angles), -weights[:, None] * jnp.sin(angles)], axis=0
    ).astype(BF16)

    by_slot = fetch_list.transpose(0, 2, 1)
    owner_row = lax.dynamic_index_in_dim(by_slot, position, 0, keepdims=False)
    picked = synthesize(owner_row, coeff, turns, table, fields)
    fetched = lax.all_to_all(picked, "dev", split_axis=0, concat_axis=0, tiled=True)

    taps = noise_kernel.astype(BF16).astype(F32)
    band = jnp.concatenate(
        [
            jnp.zeros((scans, 1), F32),
            taps[:, ::-1],
            taps[:, 1:],
            jnp.zeros((scans, HALF_BLK), F32),
        ],
        axis=1,
    )
    strips = band_strips(band[:, None, :])
    pix = block_pix.reshape(scans, -1, TILE)
    per_slot = scan_stage(
        scan_tiles,
        block_tile,
        scan_weight,
        fetched.reshape(-1, fields, TILE),
        pix,
        strips,
    )
    returned = lax.all_to_all(
        per_slot.reshape(fetched.shape), "dev", split_axis=0, concat_axis=0, tiled=True
    )
    return owner_sum(owner_row, returned)


def solution(mesh):
    return jax.shard_map(
        local,
        mesh=mesh,
        in_specs=(
            P("half", None),
            P("dev", None, "half", None),
            P("dev", None, None),
            P(),
            P(),
            P("dev", None),
            P("dev", None),
            P("dev", None),
            P("dev", None),
            P("dev"),
        ),
        out_specs=P("dev", "half", None),
        check_vma=False,
    )
```

time: 401 us -> 146 us (0.36)
  waiting for transfers between devices: 178 us -> 35.6 us
  other arithmetic: 80.8 us -> 5.42 us
  local copies, waits for them, and re-layouts: 73.5 us -> 4.86 us
  Pallas kernels: 0 us -> 40.5 us
  blocking collectives: 0 us -> 37.3 us
  matrix products: 25.8 us -> 0 us
  between operations: 14 us -> 0.14 us
    all_gather x2 -> x0, waiting for transfers between devices: 113 us -> none  [the longest x1 92.8 us: local(): every_tile = lax.all_gather(map_tiles, 'dev', axis=0, tiled=True)]
    another operation x8 -> x4, other arithmetic: 75.2 us -> 4.05 us
    pallas_call x0 -> x6, Pallas kernels: none -> 40.5 us  [the longest x1 22.4 us: scan_stage(): pl.pallas_call(scan_kernel, grid=(scans,), out_shape=jax.ShapeDtypeStruct...]
    all_to_all x0 -> x1, blocking collectives: none -> 37.3 us  [local(): lax.all_to_all(per_slot.reshape(fetched.shape), 'dev', split_axis=0, conc...]
    all_to_all x2, waiting for transfers between devices: 63.7 us -> 35.6 us  [the longest x1 25.7 us: local(): lax.all_to_all(picked, 'dev', split_axis=0, concat_axis=0, tiled=True)]
    dot_general x17 -> x0, matrix products: 25.8 us -> none  [the longest x1 5.34 us: local(): jnp.einsum('sbfp,sbpt->sbft', block_tiles, one_hot, preferred_element_typ...]
    unnamed x32 -> x17, local copies, waits for them, and re-layouts: 24.7 us -> 3.01 us
    reshape x4 -> x1, local copies, waits for them, and re-layouts: 21 us -> 0.08 us  [local(): ids = order_ids.reshape(devices, slots).T]
  transfers between devices with their start and end apart: 4 -> 3, of which waited for: 4 -> 2; matrix products, arithmetic and copies ran while one was open for 13% -> 5% of each run, Pallas kernels for 0% -> 2%
where the time goes in v1:
time: 146 us
  Pallas kernels  40.5 us (28%)
  blocking collectives  37.3 us (26%)
  waiting for transfers between devices  35.6 us (24%)
  starting transfers between devices  21.7 us (15%)
  other arithmetic  5.42 us (4%)
  local copies, waits for them, and re-layouts  4.86 us (3%)
    all_to_all x1, blocking collectives, local(): lax.all_to_all(per_slot.reshape(fetched.shape), 'dev', split_axis=0, conc...  37.3 us
    all_to_all x1, waiting for transfers between devices, local(): lax.all_to_all(picked, 'dev', split_axis=0, concat_axis=0, tiled=True)  25.7 us
    pallas_call x1, Pallas kernels, scan_stage(): pl.pallas_call(scan_kernel, grid=(scans,), out_shape=jax.ShapeDtypeStruct...  22.4 us
    all_to_all x1, starting transfers between devices, local(): coeff = lax.all_to_all(sent, 'dev', split_axis=0, concat_axis=0, tiled=True)  15 us
    all_to_all x1, waiting for transfers between devices, local(): coeff = lax.all_to_all(sent, 'dev', split_axis=0, concat_axis=0, tiled=True)  9.86 us
    all_to_all x1, starting transfers between devices, local(): lax.all_to_all(picked, 'dev', split_axis=0, concat_axis=0, tiled=True)  6.63 us
    pallas_call x1, Pallas kernels, mix_fields(): pl.pallas_call(mix_kernel, out_shape=jax.ShapeDtypeStruct((cycles, rows /...  3.99 us
    pallas_call x1, Pallas kernels, synthesize(): pl.pallas_call(synth_kernel, out_shape=jax.ShapeDtypeStruct((devices, cap...  3.95 us
  transfers between devices with their start and end apart: 3, of which 2 were waited for; matrix products, arithmetic and copies ran while one was open for 5% of the time, Pallas kernels for 2%

profile of v1, /device:TPU:32, one launch (start us, length us, event | category | flops | bytes accessed | tf_op | source)
XLA Modules:
  0.0 145.5 jit_solution(5727481727956548540)
XLA Ops:
  0.0 0.0 copy-start
  0.0 0.0 copy-start.7
  0.0 0.0 copy-start.5
  0.0 3.6 %contract_ells.1.own_ref = f32[256,128]{1,0:T(8,128)} custom-call(bf16[8,32,2048]{2,1,0:T(8,128)(2,1)} %bitcast.23, bf16[8,2048,128]{2,1,0:T(8,128)(2,1)} %leg_hbm.1), custom_call_target="tpu_custom_call" | custom-call | tf_op jit(solution)/shard_map/contract_ells/pallas_call | solution.py:41
  3.6 0.0 copy-start.6
  3.7 0.0 copy-start.3
  3.7 0.1 collective-permute-start
  3.8 0.0 copy-done.7
  3.8 0.1 reshape.94
  3.9 0.5 fusion.10
  4.5 2.6 %multiply_convert_fusion.1 = (bf16[1024,128]{1,0:T(8,128)(2,1)S(1)}, bf16[1024,128]{1,0:T(8,128)(2,1)S(1)}) fusion(s32[128]{0:T(128)S(1)} %multiply_add_fusion, s32[1024]{0:T(1024)S(1)} %bitcast.26, f32[1024]{0:T(1024)S(1)} %get-tuple-element.9, f32[1024]{0:T(1024)S(1)} %get-tuple-element.10), kind=kLoop, calls=%fused_computation.10 | loop fusion | flops 2359296 | bytes 537088 | tf_op jit(solution)/shard_map/convert
  7.1 0.8 pad_maximum_fusion.table_ref
  7.9 0.0 copy-done.5
  7.9 0.1 select_bitcast_fusion.1
  8.0 0.6 pad_maximum_fusion.2.mix_ref
  8.6 0.0 collective-permute-done.other_ref
  8.6 0.0 copy-start.4
  8.7 0.7 copy-done.4
  9.3 4.0 %mix_fields.1 = bf16[128,2,128]{2,1,0:T(2,128)(2,1)} custom-call(f32[256,128]{1,0:T(8,128)} %contract_ells.1.own_ref, f32[256,128]{1,0:T(8,128)} %copy-done.4, f32[2,16,16]{2,1,0:T(8,128)} %pad_maximum_fusion.2.mix_ref), custom_call_target="tpu_custom_call" | custom-call | tf_op jit(solution)/shard_map/mix_fields/pallas_call | solution.py:89
  13.3 15.0 %all-to-all-start = ((bf16[128,2,128]{2,1,0:T(2,128)(2,1)}), bf16[128,2,128]{2,1,0:T(2,128)(2,1)S(1)}, u32[]{:S(2)}, u32[]{:S(2)}) async-start(bf16[128,2,128]{2,1,0:T(2,128)(2,1)} %mix_fields.1), calls=%async_computation | async-start | bytes 131072 | tf_op jit(solution)/shard_map/all_to_all | solution.py:342
  28.3 0.0 copy-done
  28.3 0.6 dynamic-slice_bitcast_fusion.owner_ref
  28.9 0.7 pad_maximum_fusion.1.turn_ref
  29.6 9.9 %all-to-all-done.coeff_ref = bf16[128,2,128]{2,1,0:T(2,128)(2,1)S(1)} async-done(((bf16[128,2,128]{2,1,0:T(2,128)(2,1)}), bf16[128,2,128]{2,1,0:T(2,128)(2,1)S(1)}, u32[]{:S(2)}, u32[]{:S(2)}) %all-to-all-start) | async-done | bytes 65568 | tf_op jit(solution)/shard_map/all_to_all | solution.py:342
  39.5 0.0 copy-start.2
  39.5 0.6 copy-done.2
  40.1 4.0 %synthesize.1 = bf16[128,2,16,128]{3,2,1,0:T(8,128)(2,1)} custom-call(s32[2,128]{1,0:T(2,128)} %dynamic-slice_bitcast_fusion.owner_ref, bf16[128,2,128]{2,1,0:T(2,128)(2,1)} %copy-done.2, f32[2,32,8,128]{3,2,1,0:T(8,128)} %pad_maximum_fusion.1.turn_ref, bf16[2048,128]{1,0:T(8,128)(2,1)} %pad_maximum_fusion.table_ref), custom_call_target="tpu_custom_call" | custom-call | tf_op jit(solution)/shard_map/synthesize/pallas_call | solution.py:136
  44.1 6.6 %all-to-all-start.1 = ((bf16[128,2,16,128]{3,2,1,0:T(8,128)(2,1)}), bf16[128,2,16,128]{3,2,1,0:T(8,128)(2,1)S(1)}, u32[]{:S(2)}, u32[]{:S(2)}) async-start(bf16[128,2,16,128]{3,2,1,0:T(8,128)(2,1)} %synthesize.1), calls=%async_computation.1 | async-start | bytes 2097152 | tf_op jit(solution)/shard_map/all_to_all | solution.py:362
  50.7 0.0 copy-done.6
  50.7 0.1 slice.12
  50.8 0.4 rev.3
  51.1 0.1 concatenate.8
  51.3 0.6 broadcast_in_dim.22.row_ref
  51.9 0.0 copy-done.3
  51.9 0.7 copy.16
  52.6 3.4 %band_strips.1.strip_ref = bf16[4,256,1280]{2,1,0:T(8,128)(2,1)} custom-call(f32[4,1,1280]{2,1,0:T(1,128)} %broadcast_in_dim.22.row_ref), custom_call_target="tpu_custom_call" | custom-call | tf_op jit(solution)/shard_map/band_strips/pallas_call | solution.py:162
  56.0 25.7 %all-to-all-done.1 = bf16[128,2,16,128]{3,2,1,0:T(8,128)(2,1)S(1)} async-done(((bf16[128,2,16,128]{3,2,1,0:T(8,128)(2,1)}), bf16[128,2,16,128]{3,2,1,0:T(8,128)(2,1)S(1)}, u32[]{:S(2)}, u32[]{:S(2)}) %all-to-all-start.1) | async-done | bytes 1048608 | tf_op jit(solution)/shard_map/all_to_all | solution.py:362
  81.7 0.0 copy-start.1
  81.7 1.0 copy-done.1
  82.7 22.4 %scan_stage.1 = bf16[256,16,128]{2,1,0:T(8,128)(2,1)} custom-call(s32[4,32]{1,0:T(4,128)} %list_ref.1, s32[4,32]{1,0:T(4,128)} %entry_ref.1, f32[4]{0:T(128)} %weight_ref.1, bf16[256,16,128]{2,1,0:T(8,128)(2,1)} %bitcast.20, s32[4,128,128]{2,1,0:T(8,128)} %bitcast.22, bf16[4,256,1280]{2,1,0:T(8,128)(2,1)} %band_strips.1.strip_ref), custom_call_target="tpu_custom_call" | custom-call | tf_op jit(solution)/shard_map/scan_stage/pallas_call | solution.py:256
  105.1 37.3 %all_to_all.15.back_ref = bf16[128,2,16,128]{3,2,1,0:T(8,128)(2,1)} all-to-all(bf16[128,2,16,128]{3,2,1,0:T(8,128)(2,1)} %bitcast.21), channel_id=1, replica_groups=mesh['half'=2,'dev'=128] {'dev'}, dimensions={0} | all-to-all | bytes 2097152 | tf_op jit(solution)/shard_map/all_to_all | solution.py:384
  142.4 3.1 %owner_sum.1 = f32[1,16,4096]{2,1,0:T(8,128)} custom-call(s32[2,128]{1,0:T(2,128)} %dynamic-slice_bitcast_fusion.owner_ref, bf16[128,2,16,128]{3,2,1,0:T(8,128)(2,1)} %all_to_all.15.back_ref), custom_call_target="tpu_custom_call" | custom-call | tf_op jit(solution)/shard_map/owner_sum/pallas_call | solution.py:304
  (6 shorter events, 0.1 us)
Async XLA Ops:
  0.0 28.3 %copy-start = (s32[128,128,2]{1,2,0:T(2,128)S(1)}, s32[128,128,2]{1,2,0:T(2,128)}, u32[]{:S(2)}) copy-start(s32[128,128,2]{1,2,0:T(2,128)} %param.14) | copy-start | bytes 393220
  0.0 3.8 %copy-start.7 = (s32[1024]{0:T(1024)S(1)}, s32[1024]{0:T(1024)}, u32[]{:S(2)}) copy-start(s32[1024]{0:T(1024)} %param.13) | copy-start | bytes 12292
  0.0 7.9 %copy-start.5 = (f32[16,32]{1,0:T(8,128)S(1)}, f32[16,32]{1,0:T(8,128)}, u32[]{:S(2)}) copy-start(f32[16,32]{1,0:T(8,128)} %param.10) | copy-start | bytes 6148
  3.6 47.1 %copy-start.6 = (f32[4,512]{1,0:T(4,128)S(1)}, f32[4,512]{1,0:T(4,128)}, u32[]{:S(2)}) copy-start(f32[4,512]{1,0:T(4,128)} %param.18) | copy-start | bytes 24580
  3.7 48.2 %copy-start.3 = (s32[4,16384]{1,0:T(4,128)S(1)}, s32[4,16384]{1,0:T(4,128)}, u32[]{:S(2)}) copy-start(s32[4,16384]{1,0:T(4,128)} %param.17) | copy-start | bytes 786436
  3.7 5.0 %collective-permute-start = (f32[256,128]{1,0:T(8,128)}, f32[256,128]{1,0:T(8,128)S(1)}, u32[]{:S(2)}, u32[]{:S(2)}) collective-permute-start(f32[256,128]{1,0:T(8,128)} %contract_ells.1.own_ref), channel_id=1, source_target_pairs={{0,128},{128,0},{1,129},{129,1},{2,130},{130,2},{3,131},{131,3},{4... | collective-permute-start | bytes 393224 | tf_op jit(solution)/shard_map/ppermute | solution.py:336
  8.6 0.7 copy-start.4
  13.3 26.2 %all-to-all-start = ((bf16[128,2,128]{2,1,0:T(2,128)(2,1)}), bf16[128,2,128]{2,1,0:T(2,128)(2,1)S(1)}, u32[]{:S(2)}, u32[]{:S(2)}) async-start(bf16[128,2,128]{2,1,0:T(2,128)(2,1)} %mix_fields.1), calls=%async_computation | async-start | bytes 131072 | tf_op jit(solution)/shard_map/all_to_all | solution.py:342
  39.5 0.6 copy-start.2
  44.1 37.7 %all-to-all-start.1 = ((bf16[128,2,16,128]{3,2,1,0:T(8,128)(2,1)}), bf16[128,2,16,128]{3,2,1,0:T(8,128)(2,1)S(1)}, u32[]{:S(2)}, u32[]{:S(2)}) async-start(bf16[128,2,16,128]{3,2,1,0:T(8,128)(2,1)} %synthesize.1), calls=%async_computation.1 | async-start | bytes 2097152 | tf_op jit(solution)/shard_map/all_to_all | solution.py:362
  81.7 1.0 copy-start.1

commit v2 on v1

--- a/solution.py
+++ b/solution.py
@@ -13,11 +13,28 @@
 HALF_BLK = 256
 F32 = jnp.float32
 BF16 = jnp.bfloat16
-VMEM_LIMIT = 60 * 1024 * 1024
-
-
-def legendre_kernel(alm_hbm, leg_hbm, out_ref, alm_buf, leg_buf, sems):
-    orders = leg_buf.shape[0]
+VMEM_LIMIT = 24 * 1024 * 1024
+
+
+def cos_sin(k):
+    quarter = jnp.floor(k * (1.0 / 2048.0) + 0.5)
+    y = (k - 2048.0 * quarter) * (math.pi / NPHI)
+    y2 = y * y
+    sine = y * (1.0 + y2 * (-1.0 / 6.0 + y2 * (1.0 / 120.0 + y2 * (-1.0 / 5040.0))))
+    cosine = 1.0 + y2 * (
+        -0.5 + y2 * (1.0 / 24.0 + y2 * (-1.0 / 720.0 + y2 * (1.0 / 40320.0)))
+    )
+    turn = quarter - 4.0 * jnp.floor(quarter * 0.25)
+    odd = (turn == 1.0) | (turn == 3.0)
+    cos_sign = jnp.where((turn == 1.0) | (turn == 2.0), -1.0, 1.0)
+    sin_sign = jnp.where(turn >= 2.0, -1.0, 1.0)
+    return jnp.where(odd, sine, cosine) * cos_sign, jnp.where(odd, cosine, sine) * sin_sign
+
+
+def legendre_kernel(
+    ids_ref, alm_hbm, leg_hbm, out_ref, turn_ref, table_ref, alm_buf, leg_buf, sems
+):
+    orders, devices = ids_ref.shape
     copies = []
     for s in range(orders):
         a = pltpu.make_async_copy(alm_hbm.at[s], alm_buf.at[s], sems.at[0, s])
@@ -25,6 +42,18 @@
         a.start()
         b.start()
         copies.append((a, b))
+    ids = ids_ref[...].astype(F32)
+    tiles = turn_ref.shape[1]
+    for j in range(tiles):
+        turn_ref[0, j], turn_ref[1, j] = cos_sin(ids * float(j * 2 * NPHI // tiles))
+    odd_pixel = (2 * lax.broadcasted_iota(jnp.int32, (devices, TILE), 1) + 1).astype(F32)
+    scale = 1.0 / math.sqrt(2.0 * orders * devices)
+    for s in range(orders):
+        m = jnp.broadcast_to(ids[s : s + 1, :], (TILE, devices)).T
+        cosine, sine = cos_sin(m * odd_pixel)
+        weight = jnp.where(m == 0.0, scale, 2.0 * scale)
+        table_ref[pl.ds(s * devices, devices), :] = (weight * cosine).astype(BF16)
+        table_ref[pl.ds((orders + s) * devices, devices), :] = (-weight * sine).astype(BF16)
     for s in range(orders):
         copies[s][0].wait()
         copies[s][1].wait()
@@ -34,14 +63,24 @@
         )
 
 
-def contract_ells(alm, legendre):
+def contract_ells(ids, alm, legendre):
     orders, parts, fields, ells = alm.shape
     cycles = legendre.shape[2]
+    devices = ids.shape[1]
     rows = parts * fields
+    tiles = NPHI // TILE
     return pl.pallas_call(
         legendre_kernel,
-        out_shape=jax.ShapeDtypeStruct((orders * rows, cycles), F32),
-        in_specs=[pl.BlockSpec(memory_space=pl.ANY), pl.BlockSpec(memory_space=pl.ANY)],
+        out_shape=(
+            jax.ShapeDtypeStruct((orders * rows, cycles), F32),
+            jax.ShapeDtypeStruct((2, tiles, orders, devices), F32),
+            jax.ShapeDtypeStruct((2 * orders * devices, TILE), BF16),
+        ),
+        in_specs=[
+            pl.BlockSpec(memory_space=pltpu.VMEM),
+            pl.BlockSpec(memory_space=pl.ANY),
+            pl.BlockSpec(memory_space=pl.ANY),
+        ],
         scratch_shapes=[
             pltpu.VMEM((orders, rows, ells), BF16),
             pltpu.VMEM((orders, ells, cycles), BF16),
@@ -49,52 +88,76 @@
         ],
         compiler_params=pltpu.CompilerParams(vmem_limit_bytes=VMEM_LIMIT),
         name="contract_ells",
-    )(alm.reshape(orders, rows, ells), legendre)
-
-
-def mix_kernel(own_ref, other_ref, mix_ref, out_ref):
-    fields = mix_ref.shape[1]
+    )(
+        ids,
+        pltpu.with_memory_space_constraint(alm.reshape(orders, rows, ells), pltpu.HBM),
+        pltpu.with_memory_space_constraint(legendre, pltpu.HBM),
+    )
+
+
+def split_bf16(x):
+    high = x.astype(BF16)
+    return high, (x - high.astype(F32)).astype(BF16)
+
+
+def mix_kernel(half_ref, own_ref, other_ref, mix_ref, out_ref):
+    fields = mix_ref.shape[0]
     rows = own_ref.shape[0]
-    highest = lax.Precision.HIGHEST
-    row_group = lax.broadcasted_iota(jnp.int32, (rows, rows), 0) // fields
-    col_group = lax.broadcasted_iota(jnp.int32, (rows, rows), 1) // fields
-    spread = (
-        lax.broadcasted_iota(jnp.int32, (rows, fields), 0) % fields
-        == lax.broadcasted_iota(jnp.int32, (rows, fields), 1)
-    ).astype(F32)
-    spread_t = (
-        lax.broadcasted_iota(jnp.int32, (fields, rows), 1) % fields
-        == lax.broadcasted_iota(jnp.int32, (fields, rows), 0)
-    ).astype(F32)
-
-    def mixed(mix, values):
-        wide = jnp.dot(
-            jnp.dot(spread, mix, precision=highest, preferred_element_type=F32),
-            spread_t,
-            precision=highest,
-            preferred_element_type=F32,
-        )
-        wide = jnp.where(row_group == col_group, wide, 0.0)
-        return jnp.dot(wide, values, precision=highest, preferred_element_type=F32)
-
-    total = mixed(mix_ref[0], own_ref[...]) + mixed(mix_ref[1], other_ref[...])
+    repeats = rows // fields
+    low, high = mix_ref[:, :fields], mix_ref[:, fields:]
+    first = half_ref[0] == 0
+    same_group = (
+        lax.broadcasted_iota(jnp.int32, (rows, rows), 0) // fields
+        == lax.broadcasted_iota(jnp.int32, (rows, rows), 1) // fields
+    )
+
+    def spread(mix):
+        wide = jnp.concatenate([mix] * repeats, axis=1)
+        wide = jnp.concatenate([wide] * repeats, axis=0)
+        return split_bf16(jnp.where(same_group, wide, 0.0))
+
+    total = None
+    for mix, values in (
+        (jnp.where(first, low, high), own_ref),
+        (jnp.where(first, high, low), other_ref),
+    ):
+        mix_high, mix_low = spread(mix)
+        val_high, val_low = split_bf16(values[...])
+        for x, y in ((mix_high, val_high), (mix_high, val_low), (mix_low, val_high)):
+            term = jnp.dot(x, y, preferred_element_type=F32)
+            total = term if total is None else total + term
     by_cycle = total.T.astype(BF16)
     lanes = out_ref.shape[2]
     for p in range(out_ref.shape[1]):
         out_ref[:, p, :] = by_cycle[:, p * lanes : (p + 1) * lanes]
 
 
-def mix_fields(own, other, mix_pair):
+def mix_fields(half, own, other, field_mix):
     rows, cycles = own.shape
+    vmem = pl.BlockSpec(memory_space=pltpu.VMEM)
     return pl.pallas_call(
         mix_kernel,
         out_shape=jax.ShapeDtypeStruct((cycles, rows // 128, 128), BF16),
+        in_specs=[pl.BlockSpec(memory_space=pltpu.SMEM), vmem, vmem, vmem],
         compiler_params=pltpu.CompilerParams(vmem_limit_bytes=VMEM_LIMIT),
         name="mix_fields",
-    )(own, other, mix_pair)
-
-
-def synth_kernel(owner_ref, coeff_ref, turn_ref, table_ref, out_ref, lhs_ref, map_ref):
+    )(half, own, other, field_mix)
+
+
+def synth_kernel(
+    position_ref,
+    list_ref,
+    coeff_ref,
+    turn_ref,
+    table_ref,
+    out_ref,
+    lhs_ref,
+    map_ref,
+    owner_ref,
+    sem,
+):
+    row_copy = pltpu.make_async_copy(list_ref.at[position_ref[0]], owner_ref, sem)
+    row_copy.start()
     devices, groups, lanes = coeff_ref.shape
     tiles, fields = map_ref.shape[0], map_ref.shape[1]
     slots = turn_ref.shape[2]
@@ -119,6 +182,7 @@
     pixels = jnp.dot(lhs_ref[...], table_ref[...], preferred_element_type=F32).astype(BF16)
     map_ref[...] = pixels.reshape(tiles, fields, TILE)
     capacity = out_ref.shape[1]
+    row_copy.wait()
 
     def pick(e, carry):
         for k in range(capacity):
@@ -129,8 +193,8 @@
     lax.fori_loop(0, out_ref.shape[0], pick, 0, unroll=8)
 
 
-def synthesize(owner_row, coeff, turns, table, fields):
-    capacity, devices = owner_row.shape
+def synthesize(position, by_slot, coeff, turns, table, fields):
+    devices, capacity, _ = by_slot.shape
     tiles = turns.shape[1]
     k_total = table.shape[0]
     return pl.pallas_call(
@@ -138,6 +202,7 @@
         out_shape=jax.ShapeDtypeStruct((devices, capacity, fields, TILE), BF16),
         in_specs=[
             pl.BlockSpec(memory_space=pltpu.SMEM),
+            pl.BlockSpec(memory_space=pl.ANY),
             pl.BlockSpec(memory_space=pltpu.VMEM),
             pl.BlockSpec(memory_space=pltpu.VMEM),
             pl.BlockSpec(memory_space=pltpu.VMEM),
@@ -145,10 +210,12 @@
         scratch_shapes=[
             pltpu.VMEM((tiles * fields, k_total), BF16),
             pltpu.VMEM((tiles, fields, TILE), BF16),
+            pltpu.SMEM((capacity, devices), jnp.int32),
+            pltpu.SemaphoreType.DMA,
         ],
         compiler_params=pltpu.CompilerParams(vmem_limit_bytes=VMEM_LIMIT),
         name="synthesize",
-    )(owner_row, coeff, turns, table)
+    )(position, by_slot, coeff, turns, table)
 
 
 def band_kernel(row_ref, out_ref):
@@ -212,7 +279,7 @@
             ).astype(BF16)
         return carry
 
-    lax.fori_loop(0, blocks, gather, 0, unroll=4)
+    lax.fori_loop(0, blocks, gather, 0, unroll=16)
     total = None
     for d in range(-2, 3):
         term = jnp.dot(
@@ -222,24 +289,29 @@
         )
         total = term if total is None else total + term
     wtd_ref[...] = (weight_ref[n] * total).astype(BF16)
-    pixel_iota = lax.broadcasted_iota(jnp.int32, (TILE, TILE), 0)
+    packed = 16
+    pixel_iota = lax.broadcasted_iota(jnp.int32, (TILE, TILE), 0).astype(F32).astype(BF16)
+    one, zero = jnp.asarray(1, BF16), jnp.asarray(0, BF16)
+
+    def one_hot(b, q):
+        row = pix_ref[0, pl.ds(b * quarters + q, 1), :]
+        row = jnp.broadcast_to(row, (packed, TILE)).astype(F32).astype(BF16)
+        return jnp.where(pixel_iota == jnp.concatenate([row] * (TILE // packed), axis=0), one, zero)
 
     def bin_block(b, carry):
         slot = list_ref[n, entry_ref[n, b]]
-        partial = None
-        for q in range(quarters):
-            row = pix_ref[0, pl.ds(b * quarters + q, 1), :]
-            hot = (pixel_iota == row).astype(F32).astype(BF16)
-            start = pl.multiple_of((2 * b + q // per_half) * fields, fields)
-            values = wtd_ref[pl.ds(start, fields), pl.ds((q % per_half) * TILE, TILE)]
-            term = lax.dot_general(
-                values, hot, (((1,), (1,)), ((), ())), preferred_element_type=F32
-            )
-            partial = term if partial is None else partial + term
+        hot = jnp.concatenate([one_hot(b, q) for q in range(quarters)], axis=1)
+        start = pl.multiple_of(2 * b * fields, fields)
+        values = jnp.concatenate(
+            [wtd_ref[pl.ds(start + h * fields, fields), :] for h in range(2)], axis=1
+        )
+        partial = lax.dot_general(
+            values, hot, (((1,), (1,)), ((), ())), preferred_element_type=F32
+        )
         sum_ref[slot] = sum_ref[slot] + partial
         return carry
 
-    lax.fori_loop(0, blocks, bin_block, 0, unroll=4)
+    lax.fori_loop(0, blocks, bin_block, 0, unroll=16)
 
     @pl.when(n == pl.num_programs(0) - 1)
     def _():
@@ -278,37 +350,53 @@
     )(scan_tiles, block_tile, scan_weight, tiles, pix, strips)
 
 
-def owner_kernel(owner_ref, back_ref, out_ref, sum_ref):
+def owner_kernel(position_ref, list_ref, back_ref, out_ref, owner_ref, sem, *sum_refs):
+    row_copy = pltpu.make_async_copy(list_ref.at[position_ref[0]], owner_ref, sem)
+    row_copy.start()
     capacity, devices = owner_ref.shape
-    tiles = sum_ref.shape[1] - 1
-    sum_ref[...] = jnp.zeros_like(sum_ref)
-
-    def add(e, carry):
-        for k in range(capacity):
-            g = owner_ref[k, e]
-            g = jnp.where(g < 0, tiles, g)
-            sum_ref[k, g] = sum_ref[k, g] + back_ref[e, k].astype(F32)
+    tiles = sum_refs[0].shape[0] - 1
+    lanes = len(sum_refs) // capacity
+    for ref in sum_refs:
+        ref[...] = jnp.zeros_like(ref)
+    row_copy.wait()
+
+    def add(i, carry):
+        for j in range(lanes):
+            e = i * lanes + j
+            for k in range(capacity):
+                ref = sum_refs[j * capacity + k]
+                g = owner_ref[k, e]
+                g = jnp.where(g < 0, tiles, g)
+                ref[g] = ref[g] + back_ref[e, k].astype(F32)
         return carry
 
-    lax.fori_loop(0, devices, add, 0, unroll=8)
+    lax.fori_loop(0, devices // lanes, add, 0, unroll=8)
     for g in range(tiles):
-        total = sum_ref[0, g]
-        for k in range(1, capacity):
-            total = total + sum_ref[k, g]
+        total = sum_refs[0][g]
+        for ref in sum_refs[1:]:
+            total = total + ref[g]
         out_ref[0, :, pl.ds(g * TILE, TILE)] = total
 
 
-def owner_sum(owner_row, returned):
+def owner_sum(position, by_slot, returned):
     devices, capacity, fields, _ = returned.shape
     tiles = NPHI // TILE
     return pl.pallas_call(
         owner_kernel,
         out_shape=jax.ShapeDtypeStruct((1, fields, NPHI), F32),
-        in_specs=[pl.BlockSpec(memory_space=pltpu.SMEM), pl.BlockSpec(memory_space=pltpu.VMEM)],
-        scratch_shapes=[pltpu.VMEM((capacity, tiles + 1, fields, TILE), F32)],
+        in_specs=[
+            pl.BlockSpec(memory_space=pltpu.SMEM),
+            pl.BlockSpec(memory_space=pl.ANY),
+            pl.BlockSpec(memory_space=pltpu.VMEM),
+        ],
+        scratch_shapes=[
+            pltpu.SMEM((capacity, devices), jnp.int32),
+            pltpu.SemaphoreType.DMA,
+        ]
+        + [pltpu.VMEM((tiles + 1, fields, TILE), F32)] * (2 * capacity),
         compiler_params=pltpu.CompilerParams(vmem_limit_bytes=VMEM_LIMIT),
         name="owner_sum",
-    )(owner_row, returned)
+    )(position, by_slot, returned)
 
 
 def local(
@@ -323,42 +411,22 @@
     noise_kernel,
     scan_weight,
 ):
-    half = lax.axis_index("half")
-    position = lax.axis_index("dev")
+    half = lax.axis_index("half").reshape(1)
+    position = lax.axis_index("dev").reshape(1)
     devices = fetch_list.shape[0]
     fields = alm.shape[2]
     slots = alm.shape[0]
-    order_count = order_ids.shape[0]
     scans = block_pix.shape[0]
-    tile_count = NPHI // TILE
-
-    own = contract_ells(alm, legendre)
+
+    ids = order_ids.reshape(devices, slots).T
+    own, turns, table = contract_ells(ids, alm, legendre)
     other = lax.ppermute(own, "half", [(0, 1), (1, 0)])
-    low, high = field_mix[:, :fields], field_mix[:, fields:]
-    mix_pair = jnp.stack(
-        [jnp.where(half == 0, low, high), jnp.where(half == 0, high, low)], axis=0
-    )
-    sent = mix_fields(own, other, mix_pair)
+    sent = mix_fields(half, own, other, field_mix)
     coeff = lax.all_to_all(sent, "dev", split_axis=0, concat_axis=0, tiled=True)
 
-    ids = order_ids.reshape(devices, slots).T
-    tile_iota = jnp.arange(tile_count, dtype=jnp.int32)
-    turn_angle = ((ids[None] * tile_iota[:, None, None]) % tile_count).astype(F32) * (
-        2.0 * math.pi / tile_count
-    )
-    turns = jnp.stack([jnp.cos(turn_angle), jnp.sin(turn_angle)], axis=0)
-    flat_ids = ids.reshape(-1)
-    pixel_iota = jnp.arange(TILE, dtype=jnp.int32)
-    steps = flat_ids[:, None] * (2 * pixel_iota[None, :] + 1) % (2 * NPHI)
-    angles = steps.astype(F32) * (math.pi / NPHI)
-    weights = jnp.where(flat_ids == 0, 1.0, 2.0).astype(F32) / math.sqrt(2.0 * order_count)
-    table = jnp.concatenate(
-        [weights[:, None] * jnp.cos(angles), -weights[:, None] * jnp.sin(angles)], axis=0
-    ).astype(BF16)
-
     by_slot = fetch_list.transpose(0, 2, 1)
-    owner_row = lax.dynamic_index_in_dim(by_slot, position, 0, keepdims=False)
-    picked = synthesize(owner_row, coeff, turns, table, fields)
+    picked = synthesize(position, by_slot, coeff, turns, table, fields)
+    picked, noise_kernel, block_pix = lax.optimization_barrier((picked, noise_kernel, block_pix))
     fetched = lax.all_to_all(picked, "dev", split_axis=0, concat_axis=0, tiled=True)
 
     taps = noise_kernel.astype(BF16).astype(F32)
@@ -384,7 +452,7 @@
     returned = lax.all_to_all(
         per_slot.reshape(fetched.shape), "dev", split_axis=0, concat_axis=0, tiled=True
     )
-    return owner_sum(owner_row, returned)
+    return owner_sum(position, by_slot, returned)
 
 
 def solution(mesh):

time: 146 us -> 124 us (0.85)
  Pallas kernels: 40.5 us -> 22.1 us
  waiting for transfers between devices: 35.6 us -> 41.4 us
  other arithmetic: 5.42 us -> 0.01 us
  local copies, waits for them, and re-layouts: 4.86 us -> 1.45 us
  blocking collectives: 37.3 us -> 35.4 us
    pallas_call x1, Pallas kernels: 22.4 us -> 12.2 us  [scan_stage(): pl.pallas_call(scan_kernel, grid=(scans,), out_shape=jax.ShapeDtypeStruct...]
    another operation x4 -> x0, other arithmetic: 4.05 us -> none
    all_to_all x1, waiting for transfers between devices: 25.7 us -> 29 us  [local(): lax.all_to_all(picked, 'dev', split_axis=0, concat_axis=0, tiled=True)]
    unnamed x17 -> x15, local copies, waits for them, and re-layouts: 3.01 us -> 0.05 us
    pallas_call x1, Pallas kernels: 3.4 us -> 0.69 us  [band_strips(): pl.pallas_call(band_kernel, grid=(scans,), out_shape=jax.ShapeDtypeStruct...]
    pallas_call x1, Pallas kernels: 3.99 us -> 1.33 us  [mix_fields(): pl.pallas_call(mix_kernel, out_shape=jax.ShapeDtypeStruct((cycles, rows /...]
    all_to_all x1, blocking collectives: 37.3 us -> 35.4 us  [local(): lax.all_to_all(per_slot.reshape(fetched.shape), 'dev', split_axis=0, conc...]
  transfers between devices with their start and end apart: 3 -> 3, of which waited for: 2 -> 3; matrix products, arithmetic and copies ran while one was open for 5% -> 0% of each run, Pallas kernels for 2% -> 1%
where the time goes in v2:
time: 124 us; the launch traced here: 123 us
  waiting for transfers between devices  41.4 us (33%)
  blocking collectives  35.4 us (29%)
  starting transfers between devices  22.8 us (18%)
  Pallas kernels  22.1 us (18%)
  local copies, waits for them, and re-layouts  1.45 us (1%)
    all_to_all x1, blocking collectives, local(): lax.all_to_all(per_slot.reshape(fetched.shape), 'dev', split_axis=0, conc...  35.4 us
    all_to_all x1, waiting for transfers between devices, local(): lax.all_to_all(picked, 'dev', split_axis=0, concat_axis=0, tiled=True)  29 us
    all_to_all x1, starting transfers between devices, local(): coeff = lax.all_to_all(sent, 'dev', split_axis=0, concat_axis=0, tiled=True)  15 us
    pallas_call x1, Pallas kernels, scan_stage(): pl.pallas_call(scan_kernel, grid=(scans,), out_shape=jax.ShapeDtypeStruct...  12.2 us
    all_to_all x1, waiting for transfers between devices, local(): coeff = lax.all_to_all(sent, 'dev', split_axis=0, concat_axis=0, tiled=True)  11.1 us
    all_to_all x1, starting transfers between devices, local(): lax.all_to_all(picked, 'dev', split_axis=0, concat_axis=0, tiled=True)  7.71 us
    pallas_call x1, Pallas kernels, contract_ells(): pl.pallas_call(legendre_kernel, out_shape=(jax.ShapeDtypeStruct((orders *...  3.06 us
    pallas_call x1, Pallas kernels, synthesize(): pl.pallas_call(synth_kernel, out_shape=jax.ShapeDtypeStruct((devices, cap...  2.85 us
  transfers between devices with their start and end apart: 3, of which 3 were waited for; matrix products, arithmetic and copies ran while one was open for 0% of the time, Pallas kernels for 1%

profile of v2, /device:TPU:32, one launch (start us, length us, event | category | flops | bytes accessed | tf_op | source)
XLA Modules:
  0.0 123.3 jit_solution(10768443927443416026)
XLA Ops:
  0.0 0.0 copy-start.1
  0.0 0.0 copy-start
  0.0 0.8 reshape.23
  0.9 0.0 copy-start.6
  0.9 0.0 copy-start.5
  0.9 3.1 %contract_ells.1 = (f32[256,128]{1,0:T(8,128)S(1)}, f32[2,32,8,128]{3,2,1,0:T(8,128)S(1)}, bf16[2048,128]{1,0:T(8,128)(2,1)S(1)}) custom-call(s32[8,128]{1,0:T(8,128)S(1)} %bitcast.15, bf16[8,32,2048]{2,1,0:T(8,128)(2,1)} %bitcast.16, bf16[8,2048,128]{2,1,0:T(8,128)(2,1)} %leg_hbm.1), custom_call_target="tpu_custom_call" | custom-call | tf_op jit(solution)/shard_map/contract_ells/pallas_call | solution.py:72
  3.9 0.0 copy-start.2
  3.9 0.0 copy-start.3
  4.0 0.0 copy-start.4
  4.0 0.1 collective-permute-start
  4.1 1.3 %collective-permute-done.other_ref = f32[256,128]{1,0:T(8,128)S(1)} collective-permute-done((f32[256,128]{1,0:T(8,128)S(1)}, f32[256,128]{1,0:T(8,128)S(1)}, u32[]{:S(2)}, u32[]{:S(2)}) %collective-permute-start) | collective-permute-done | bytes 131104 | tf_op jit(solution)/shard_map/ppermute | solution.py:423
  5.4 0.0 copy-done.1
  5.4 1.3 %mix_fields.1 = bf16[128,2,128]{2,1,0:T(2,128)(2,1)} custom-call(s32[1]{0:T(128)} %bitcast.2.half_ref, f32[256,128]{1,0:T(8,128)S(1)} %get-tuple-element.11.own_ref, f32[256,128]{1,0:T(8,128)S(1)} %collective-permute-done.other_ref, f32[16,32]{1,0:T(8,128)S(1)} %copy-done.1), custom_call_target="tpu_custom_call" | custom-call | tf_op jit(solution)/shard_map/mix_fields/pallas_call | solution.py:138
  6.7 15.0 %all-to-all-start = ((bf16[128,2,128]{2,1,0:T(2,128)(2,1)}), bf16[128,2,128]{2,1,0:T(2,128)(2,1)S(1)}, u32[]{:S(2)}, u32[]{:S(2)}) async-start(bf16[128,2,128]{2,1,0:T(2,128)(2,1)} %mix_fields.1), calls=%async_computation | async-start | bytes 131072 | tf_op jit(solution)/shard_map/all_to_all | solution.py:425
  21.8 11.1 %all-to-all-done.coeff_ref = bf16[128,2,128]{2,1,0:T(2,128)(2,1)S(1)} async-done(((bf16[128,2,128]{2,1,0:T(2,128)(2,1)}), bf16[128,2,128]{2,1,0:T(2,128)(2,1)S(1)}, u32[]{:S(2)}, u32[]{:S(2)}) %all-to-all-start) | async-done | bytes 65568 | tf_op jit(solution)/shard_map/all_to_all | solution.py:425
  32.9 0.0 copy-done
  32.9 2.8 %synthesize.1 = bf16[128,2,16,128]{3,2,1,0:T(8,128)(2,1)} custom-call(s32[1]{0:T(128)} %bitcast.position_ref, s32[128,2,128]{2,1,0:T(2,128)S(1)} %bitcast.13, bf16[128,2,128]{2,1,0:T(2,128)(2,1)S(1)} %all-to-all-done.coeff_ref, f32[2,32,8,128]{3,2,1,0:T(8,128)S(1)} %get-tuple-element.12.turn_ref, bf16[2048,128]{1,0:T(8,128)(2,1)S(1)} %get-tuple-element.13.table_ref), custom_call_target="tpu_custom_call" | custom-call | tf_op jit(solution)/shard_map/synthesize/pallas_call | solution.py:200
  35.7 7.7 %all-to-all-start.1 = ((bf16[128,2,16,128]{3,2,1,0:T(8,128)(2,1)}), bf16[128,2,16,128]{3,2,1,0:T(8,128)(2,1)}, u32[]{:S(2)}, u32[]{:S(2)}) async-start(bf16[128,2,16,128]{3,2,1,0:T(8,128)(2,1)} %synthesize.1), calls=%async_computation.1 | async-start | bytes 2097152 | tf_op jit(solution)/shard_map/all_to_all | solution.py:430
  43.4 0.0 copy-done.6
  43.4 0.1 slice.4
  43.5 0.4 rev.3
  43.9 0.1 concatenate.3
  44.0 0.0 copy-done.5
  44.0 0.7 band_strips.1.strip_ref
  44.7 29.0 %all-to-all-done.1 = bf16[128,2,16,128]{3,2,1,0:T(8,128)(2,1)} async-done(((bf16[128,2,16,128]{3,2,1,0:T(8,128)(2,1)}), bf16[128,2,16,128]{3,2,1,0:T(8,128)(2,1)}, u32[]{:S(2)}, u32[]{:S(2)}) %all-to-all-start.1) | async-done | bytes 1048608 | tf_op jit(solution)/shard_map/all_to_all | solution.py:430
  73.7 0.0 copy-done.2
  73.7 0.0 copy-done.3
  73.7 0.0 copy-done.4
  73.7 12.2 %scan_stage.1 = bf16[256,16,128]{2,1,0:T(8,128)(2,1)S(1)} custom-call(s32[4,32]{1,0:T(4,128)S(1)} %copy-done.2, s32[4,32]{1,0:T(4,128)S(1)} %copy-done.3, f32[4]{0:T(128)S(1)} %copy-done.4, bf16[256,16,128]{2,1,0:T(8,128)(2,1)} %bitcast.5.tiles_ref, s32[4,128,128]{2,1,0:T(8,128)S(1)} %bitcast.12, bf16[4,256,1280]{2,1,0:T(8,128)(2,1)S(1)} %band_strips.1.strip_ref), custom_call_target="tpu_custom_call" | custom-call | tf_op jit(solution)/shard_map/scan_stage/pallas_call | solution.py:328
  86.0 35.4 %all_to_all.15.back_ref = bf16[128,2,16,128]{3,2,1,0:T(8,128)(2,1)S(1)} all-to-all(bf16[128,2,16,128]{3,2,1,0:T(8,128)(2,1)S(1)} %bitcast.11), channel_id=1, replica_groups=mesh['half'=2,'dev'=128] {'dev'}, dimensions={0} | all-to-all | bytes 2097152 | tf_op jit(solution)/shard_map/all_to_all | solution.py:452
  121.4 1.9 %owner_sum.1 = f32[1,16,4096]{2,1,0:T(8,128)} custom-call(s32[1]{0:T(128)} %bitcast.position_ref, s32[128,2,128]{2,1,0:T(2,128)S(1)} %bitcast.14, bf16[128,2,16,128]{3,2,1,0:T(8,128)(2,1)S(1)} %all_to_all.15.back_ref), custom_call_target="tpu_custom_call" | custom-call | tf_op jit(solution)/shard_map/owner_sum/pallas_call | solution.py:384
  (6 shorter events, 0.1 us)
Async XLA Ops:
  0.0 5.4 %copy-start.1 = (f32[16,32]{1,0:T(8,128)S(1)}, f32[16,32]{1,0:T(8,128)}, u32[]{:S(2)}) copy-start(f32[16,32]{1,0:T(8,128)} %mix_ref.1) | copy-start | bytes 6148
  0.0 32.8 %copy-start = (s32[128,128,2]{1,2,0:T(2,128)S(1)}, s32[128,128,2]{1,2,0:T(2,128)}, u32[]{:S(2)}) copy-start(s32[128,128,2]{1,2,0:T(2,128)} %param.14) | copy-start | bytes 393220
  0.9 42.6 %copy-start.6 = (f32[4,512]{1,0:T(4,128)S(1)}, f32[4,512]{1,0:T(4,128)}, u32[]{:S(2)}) copy-start(f32[4,512]{1,0:T(4,128)} %param.18) | copy-start | bytes 24580
  0.9 43.1 %copy-start.5 = (s32[4,16384]{1,0:T(4,128)S(1)}, s32[4,16384]{1,0:T(4,128)}, u32[]{:S(2)}) copy-start(s32[4,16384]{1,0:T(4,128)} %param.17) | copy-start | bytes 786436
  3.9 69.8 %copy-start.2 = (s32[4,32]{1,0:T(4,128)S(1)}, s32[4,32]{1,0:T(4,128)}, u32[]{:S(2)}) copy-start(s32[4,32]{1,0:T(4,128)} %list_ref.1) | copy-start | bytes 1540
  3.9 69.8 %copy-start.3 = (s32[4,32]{1,0:T(4,128)S(1)}, s32[4,32]{1,0:T(4,128)}, u32[]{:S(2)}) copy-start(s32[4,32]{1,0:T(4,128)} %entry_ref.1) | copy-start | bytes 1540
  4.0 69.8 %copy-start.4 = (f32[4]{0:T(128)S(1)}, f32[4]{0:T(128)}, u32[]{:S(2)}) copy-start(f32[4]{0:T(128)} %weight_ref.1) | copy-start | bytes 52
  4.0 1.4 %collective-permute-start = (f32[256,128]{1,0:T(8,128)S(1)}, f32[256,128]{1,0:T(8,128)S(1)}, u32[]{:S(2)}, u32[]{:S(2)}) collective-permute-start(f32[256,128]{1,0:T(8,128)S(1)} %get-tuple-element.11.own_ref), channel_id=1, source_target_pairs={{0,128},{128,0},{1,129},{129,1},{2,130},{130,2},{3,131},{131,3},{4... | collective-permute-start | bytes 393224 | tf_op jit(solution)/shard_map/ppermute | solution.py:423
  6.7 26.1 %all-to-all-start = ((bf16[128,2,128]{2,1,0:T(2,128)(2,1)}), bf16[128,2,128]{2,1,0:T(2,128)(2,1)S(1)}, u32[]{:S(2)}, u32[]{:S(2)}) async-start(bf16[128,2,128]{2,1,0:T(2,128)(2,1)} %mix_fields.1), calls=%async_computation | async-start | bytes 131072 | tf_op jit(solution)/shard_map/all_to_all | solution.py:425
  35.7 38.0 %all-to-all-start.1 = ((bf16[128,2,16,128]{3,2,1,0:T(8,128)(2,1)}), bf16[128,2,16,128]{3,2,1,0:T(8,128)(2,1)}, u32[]{:S(2)}, u32[]{:S(2)}) async-start(bf16[128,2,16,128]{3,2,1,0:T(8,128)(2,1)} %synthesize.1), calls=%async_computation.1 | async-start | bytes 2097152 | tf_op jit(solution)/shard_map/all_to_all | solution.py:430

commit v3 on v2

--- a/solution.py
+++ b/solution.py
@@ -11,9 +11,13 @@
 TILE = 128
 BLK = 512
 HALF_BLK = 256
+RING = 8
+SHARE = 2
+COPIES = RING // SHARE
 F32 = jnp.float32
 BF16 = jnp.bfloat16
 VMEM_LIMIT = 24 * 1024 * 1024
+SCAN_LIMIT = 40 * 1024 * 1024
 
 
 def cos_sin(k):
@@ -34,7 +38,7 @@
 def legendre_kernel(
     ids_ref, alm_hbm, leg_hbm, out_ref, turn_ref, table_ref, alm_buf, leg_buf, sems
 ):
-    orders, devices = ids_ref.shape
+    orders, devices = turn_ref.shape[2:]
     copies = []
     for s in range(orders):
         a = pltpu.make_async_copy(alm_hbm.at[s], alm_buf.at[s], sems.at[0, s])
@@ -42,7 +46,21 @@
         a.start()
         b.start()
         copies.append((a, b))
-    ids = ids_ref[...].astype(F32)
+    flat = ids_ref[...].astype(F32)
+    lane = lax.broadcasted_iota(jnp.int32, (orders, TILE), 1)
+    slot = lax.broadcasted_iota(jnp.int32, (orders, TILE), 0)
+    spread = jnp.concatenate(
+        [jnp.where(lane % orders == slot, flat[i : i + 1, :], 0.0) for i in range(flat.shape[0])],
+        axis=1,
+    )
+    count = orders * devices
+    holder = (
+        lax.broadcasted_iota(jnp.int32, (count, devices), 0) // orders
+        == lax.broadcasted_iota(jnp.int32, (count, devices), 1)
+    ).astype(F32).astype(BF16)
+    ids = sum(
+        jnp.dot(part, holder, preferred_element_type=F32) for part in split_bf16(spread)
+    )
     tiles = turn_ref.shape[1]
     for j in range(tiles):
         turn_ref[0, j], turn_ref[1, j] = cos_sin(ids * float(j * 2 * NPHI // tiles))
@@ -66,7 +84,7 @@
 def contract_ells(ids, alm, legendre):
     orders, parts, fields, ells = alm.shape
     cycles = legendre.shape[2]
-    devices = ids.shape[1]
+    devices = ids.shape[0] // orders
     rows = parts * fields
     tiles = NPHI // TILE
     return pl.pallas_call(
@@ -89,7 +107,7 @@
         compiler_params=pltpu.CompilerParams(vmem_limit_bytes=VMEM_LIMIT),
         name="contract_ells",
     )(
-        ids,
+        ids.reshape(-1, TILE),
         pltpu.with_memory_space_constraint(alm.reshape(orders, rows, ells), pltpu.HBM),
         pltpu.with_memory_space_constraint(legendre, pltpu.HBM),
     )
@@ -126,10 +144,27 @@
         for x, y in ((mix_high, val_high), (mix_high, val_low), (mix_low, val_high)):
             term = jnp.dot(x, y, preferred_element_type=F32)
             total = term if total is None else total + term
-    by_cycle = total.T.astype(BF16)
+    rounded = total.astype(BF16)
     lanes = out_ref.shape[2]
-    for p in range(out_ref.shape[1]):
-        out_ref[:, p, :] = by_cycle[:, p * lanes : (p + 1) * lanes]
+    cycles = total.shape[1]
+    parts = rows // lanes
+    per_target = parts * COPIES
+    count = out_ref.shape[0] * per_target
+    row = lax.broadcasted_iota(jnp.int32, (count, cycles), 0)
+    target, inner = row // per_target, row % per_target
+    cycle = (target // RING) * RING + target % SHARE + SHARE * (inner % COPIES)
+    wanted = cycle == lax.broadcasted_iota(jnp.int32, (count, cycles), 1)
+    spread_out = None
+    for p in range(parts):
+        pick = (wanted & (inner // COPIES == p)).astype(F32).astype(BF16)
+        term = lax.dot_general(
+            pick,
+            rounded[p * lanes : (p + 1) * lanes],
+            (((1,), (1,)), ((), ())),
+            preferred_element_type=F32,
+        )
+        spread_out = term if spread_out is None else spread_out + term
+    out_ref[...] = spread_out.reshape(out_ref.shape).astype(BF16)
 
 
 def mix_fields(half, own, other, field_mix):
@@ -137,7 +172,7 @@
     vmem = pl.BlockSpec(memory_space=pltpu.VMEM)
     return pl.pallas_call(
         mix_kernel,
-        out_shape=jax.ShapeDtypeStruct((cycles, rows // 128, 128), BF16),
+        out_shape=jax.ShapeDtypeStruct((cycles, rows // TILE * COPIES, TILE), BF16),
         in_specs=[pl.BlockSpec(memory_space=pltpu.SMEM), vmem, vmem, vmem],
         compiler_params=pltpu.CompilerParams(vmem_limit_bytes=VMEM_LIMIT),
         name="mix_fields",
@@ -151,67 +186,96 @@
     turn_ref,
     table_ref,
     out_ref,
-    lhs_ref,
+    flip_ref,
+    even_ref,
+    odd_ref,
     map_ref,
     owner_ref,
-    sem,
+    sems,
 ):
-    row_copy = pltpu.make_async_copy(list_ref.at[position_ref[0]], owner_ref, sem)
-    row_copy.start()
-    devices, groups, lanes = coeff_ref.shape
-    tiles, fields = map_ref.shape[0], map_ref.shape[1]
+    position = position_ref[0]
+    ring_at = position % RING
+    first = position - ring_at + ring_at % SHARE
+    row_copies = [
+        pltpu.make_async_copy(list_ref.at[first + SHARE * k], owner_ref.at[k], sems.at[k])
+        for k in range(COPIES)
+    ]
+    for copy in row_copies:
+        copy.start()
+    devices = coeff_ref.shape[0]
+    groups = coeff_ref.shape[1] // COPIES
+    tiles, fields = map_ref.shape[1:3]
     slots = turn_ref.shape[2]
     per_group = slots // groups
     k_half = slots * devices
-    flipped = [coeff_ref[:, g, :].astype(F32).T for g in range(groups)]
-    for s in range(slots):
-        block = flipped[s // per_group]
-        at = (s % per_group) * 2 * fields
-        real = block[at : at + fields]
-        imag = block[at + fields : at + 2 * fields]
-        for j in range(tiles):
-            cos_row = turn_ref[0, j, s : s + 1, :]
-            sin_row = turn_ref[1, j, s : s + 1, :]
-            rows = pl.ds(j * fields, fields)
-            lhs_ref[rows, pl.ds(s * devices, devices)] = (real * cos_row - imag * sin_row).astype(
-                BF16
-            )
-            lhs_ref[rows, pl.ds(k_half + s * devices, devices)] = (
-                real * sin_row + imag * cos_row
-            ).astype(BF16)
-    pixels = jnp.dot(lhs_ref[...], table_ref[...], preferred_element_type=F32).astype(BF16)
-    map_ref[...] = pixels.reshape(tiles, fields, TILE)
-    capacity = out_ref.shape[1]
-    row_copy.wait()
-
-    def pick(e, carry):
-        for k in range(capacity):
-            g = jnp.maximum(owner_ref[k, e], 0)
-            out_ref[e, k] = map_ref[g]
+    for k in range(COPIES):
+        for g in range(groups):
+            flip_ref[k, g] = coeff_ref[:, g * COPIES + k, :].astype(F32).T
+
+    def one_cycle(k, lhs):
+        for s in range(slots):
+            at = (s % per_group) * 2 * fields
+            real = flip_ref[k, s // per_group, pl.ds(at, fields), :]
+            imag = flip_ref[k, s // per_group, pl.ds(at + fields, fields), :]
+            for j in range(tiles):
+                cos_row = turn_ref[0, j, s : s + 1, :]
+                sin_row = turn_ref[1, j, s : s + 1, :]
+                rows = pl.ds(j * fields, fields)
+                lhs[rows, pl.ds(s * devices, devices)] = (
+                    real * cos_row - imag * sin_row
+                ).astype(BF16)
+                lhs[rows, pl.ds(k_half + s * devices, devices)] = (
+                    real * sin_row + imag * cos_row
+                ).astype(BF16)
+        pixels = jnp.dot(lhs[...], table_ref[...], preferred_element_type=F32).astype(BF16)
+        map_ref[k] = pixels.reshape(tiles, fields, TILE)
+
+    def cycle_pair(i, carry):
+        for u, lhs in enumerate((even_ref, odd_ref)):
+            one_cycle(2 * i + u, lhs)
         return carry
 
-    lax.fori_loop(0, out_ref.shape[0], pick, 0, unroll=8)
+    lax.fori_loop(0, COPIES // 2, cycle_pair, 0)
+    for copy in row_copies:
+        copy.wait()
+    capacity = out_ref.shape[2]
+    base = ring_at - ring_at % SHARE
+
+    def pick(t, carry):
+        e = (t // SHARE) * RING + base + t % SHARE
+        for k in range(COPIES):
+            for c in range(capacity):
+                out_ref[t, k, c] = map_ref[k, jnp.maximum(owner_ref[k, c, e], 0)]
+        return carry
+
+    lax.fori_loop(0, out_ref.shape[0], pick, 0, unroll=2)
 
 
 def synthesize(position, by_slot, coeff, turns, table, fields):
     devices, capacity, _ = by_slot.shape
     tiles = turns.shape[1]
     k_total = table.shape[0]
+    groups = coeff.shape[1] // COPIES
+    vmem = pl.BlockSpec(memory_space=pltpu.VMEM)
     return pl.pallas_call(
         synth_kernel,
-        out_shape=jax.ShapeDtypeStruct((devices, capacity, fields, TILE), BF16),
+        out_shape=jax.ShapeDtypeStruct(
+            (devices // COPIES, COPIES, capacity, fields, TILE), BF16
+        ),
         in_specs=[
             pl.BlockSpec(memory_space=pltpu.SMEM),
             pl.BlockSpec(memory_space=pl.ANY),
-            pl.BlockSpec(memory_space=pltpu.VMEM),
-            pl.BlockSpec(memory_space=pltpu.VMEM),
-            pl.BlockSpec(memory_space=pltpu.VMEM),
+            vmem,
+            vmem,
+            vmem,
         ],
         scratch_shapes=[
+            pltpu.VMEM((COPIES, groups, TILE, devices), F32),
             pltpu.VMEM((tiles * fields, k_total), BF16),
-            pltpu.VMEM((tiles, fields, TILE), BF16),
-            pltpu.SMEM((capacity, devices), jnp.int32),
-            pltpu.SemaphoreType.DMA,
+            pltpu.VMEM((tiles * fields, k_total), BF16),
+            pltpu.VMEM((COPIES, tiles, fields, TILE), BF16),
+            pltpu.SMEM((COPIES, capacity, devices), jnp.int32),
+            pltpu.SemaphoreType.DMA((COPIES,)),
         ],
         compiler_params=pltpu.CompilerParams(vmem_limit_bytes=VMEM_LIMIT),
         name="synthesize",
@@ -237,30 +301,77 @@
     )(rows)
 
 
+def one_hot(row):
+    packed = 16
+    iota = lax.broadcasted_iota(jnp.int32, (TILE, TILE), 0).astype(F32).astype(BF16)
+    row = jnp.broadcast_to(row, (packed, TILE)).astype(F32).astype(BF16)
+    row = jnp.concatenate([row] * (TILE // packed), axis=0)
+    return jnp.where(iota == row, jnp.asarray(1, BF16), jnp.asarray(0, BF16))
+
+
+def hot_kernel(pix_ref, out_ref):
+    quarters = BLK // TILE
+
+    def body(b, carry):
+        for q in range(quarters):
+            row = pix_ref[0, pl.ds(b * quarters + q, 1), :]
+            out_ref[0, b, pl.ds(q * TILE, TILE), :] = one_hot(row).T
+        return carry
+
+    lax.fori_loop(0, out_ref.shape[1], body, 0, unroll=8)
+
+
+def hot_blocks(pix):
+    scans, rows, _ = pix.shape
+    blocks = rows * TILE // BLK
+    hots = pl.pallas_call(
+        hot_kernel,
+        grid=(scans,),
+        out_shape=jax.ShapeDtypeStruct((scans, blocks, BLK, TILE), BF16),
+        in_specs=[pl.BlockSpec((1, rows, TILE), lambda n: (n, 0, 0))],
+        out_specs=pl.BlockSpec((1, blocks, BLK, TILE), lambda n: (n, 0, 0, 0)),
+        compiler_params=pltpu.CompilerParams(vmem_limit_bytes=VMEM_LIMIT),
+        name="hot_blocks",
+    )(pix)
+    return pltpu.with_memory_space_constraint(hots, pltpu.HBM)
+
+
 def scan_kernel(
-    list_ref, entry_ref, weight_ref, tiles_ref, pix_ref, strip_ref, out_ref, pad_ref, wtd_ref, sum_ref
+    list_ref,
+    moved_ref,
+    entry_ref,
+    weight_ref,
+    tiles_ref,
+    pix_ref,
+    strip_ref,
+    hot_hbm,
+    out_ref,
+    pad_ref,
+    wtd_ref,
+    sum_ref,
+    hot_ref,
+    sems,
 ):
-    n = pl.program_id(0)
+    scans, blocks = entry_ref.shape
+    copies = [
+        pltpu.make_async_copy(hot_hbm.at[n], hot_ref.at[n], sems.at[n]) for n in range(scans)
+    ]
+    for copy in copies:
+        copy.start()
     fields = tiles_ref.shape[1]
-    blocks = entry_ref.shape[1]
     halves = 2 * blocks
     edge = 2 * fields
-
-    @pl.when(n == 0)
-    def _():
-        sum_ref[...] = jnp.zeros_like(sum_ref)
-        pad_ref[pl.ds(0, edge), :] = jnp.zeros((edge, HALF_BLK), BF16)
-        pad_ref[pl.ds(edge + halves * fields, edge), :] = jnp.zeros((edge, HALF_BLK), BF16)
-
     per_half = HALF_BLK // TILE
     quarters = BLK // TILE
-
-    def gather(b, carry):
-        slot = list_ref[n, entry_ref[n, b]]
-        tile = tiles_ref[slot].astype(F32)
+    sum_ref[...] = jnp.zeros_like(sum_ref)
+    for p in range(2):
+        pad_ref[p, pl.ds(0, edge), :] = jnp.zeros((edge, HALF_BLK), BF16)
+        pad_ref[p, pl.ds(edge + halves * fields, edge), :] = jnp.zeros((edge, HALF_BLK), BF16)
+
+    def gather(n, b):
+        tile = tiles_ref[moved_ref[n, entry_ref[n, b]]].astype(F32)
         for q in range(quarters):
-            row = pix_ref[0, pl.ds(b * quarters + q, 1), :]
-            at = jnp.broadcast_to(row, (8, TILE))
+            at = jnp.broadcast_to(pix_ref[n, pl.ds(b * quarters + q, 1), :], (8, TILE))
             live = at >= 0
             index = jnp.maximum(at, 0)
             parts = [
@@ -274,80 +385,68 @@
                 for i in range(fields // 8)
             ]
             start = pl.multiple_of(edge + (2 * b + q // per_half) * fields, fields)
-            pad_ref[pl.ds(start, fields), pl.ds((q % per_half) * TILE, TILE)] = jnp.concatenate(
-                parts, axis=0
-            ).astype(BF16)
-        return carry
-
-    lax.fori_loop(0, blocks, gather, 0, unroll=16)
-    total = None
-    for d in range(-2, 3):
-        term = jnp.dot(
-            pad_ref[pl.ds(edge - d * fields, halves * fields), :],
-            strip_ref[0, :, pl.ds((d + 2) * HALF_BLK, HALF_BLK)],
-            preferred_element_type=F32,
-        )
-        total = term if total is None else total + term
-    wtd_ref[...] = (weight_ref[n] * total).astype(BF16)
-    packed = 16
-    pixel_iota = lax.broadcasted_iota(jnp.int32, (TILE, TILE), 0).astype(F32).astype(BF16)
-    one, zero = jnp.asarray(1, BF16), jnp.asarray(0, BF16)
-
-    def one_hot(b, q):
-        row = pix_ref[0, pl.ds(b * quarters + q, 1), :]
-        row = jnp.broadcast_to(row, (packed, TILE)).astype(F32).astype(BF16)
-        return jnp.where(pixel_iota == jnp.concatenate([row] * (TILE // packed), axis=0), one, zero)
-
-    def bin_block(b, carry):
+            pad_ref[
+                n % 2, pl.ds(start, fields), pl.ds((q % per_half) * TILE, TILE)
+            ] = jnp.concatenate(parts, axis=0).astype(BF16)
+
+    def filter_scan(n):
+        total = None
+        for d in range(-2, 3):
+            term = jnp.dot(
+                pad_ref[n % 2, pl.ds(edge - d * fields, halves * fields), :],
+                strip_ref[n, :, pl.ds((d + 2) * HALF_BLK, HALF_BLK)],
+                preferred_element_type=F32,
+            )
+            total = term if total is None else total + term
+        wtd_ref[...] = (weight_ref[n] * total).astype(BF16)
+
+    def bin_block(n, b):
         slot = list_ref[n, entry_ref[n, b]]
-        hot = jnp.concatenate([one_hot(b, q) for q in range(quarters)], axis=1)
         start = pl.multiple_of(2 * b * fields, fields)
         values = jnp.concatenate(
             [wtd_ref[pl.ds(start + h * fields, fields), :] for h in range(2)], axis=1
         )
-        partial = lax.dot_general(
-            values, hot, (((1,), (1,)), ((), ())), preferred_element_type=F32
+        sum_ref[slot] = sum_ref[slot] + jnp.dot(
+            values, hot_ref[n, b], preferred_element_type=F32
         )
-        sum_ref[slot] = sum_ref[slot] + partial
-        return carry
-
-    lax.fori_loop(0, blocks, bin_block, 0, unroll=16)
-
-    @pl.when(n == pl.num_programs(0) - 1)
-    def _():
-        out_ref[...] = sum_ref[...].astype(BF16)
-
-
-def scan_stage(scan_tiles, block_tile, scan_weight, tiles, pix, strips):
+
+    def run(body):
+        lax.fori_loop(0, blocks, lambda b, carry: (body(b), carry)[1], 0, unroll=16)
+
+    run(lambda b: gather(0, b))
+    for n in range(scans):
+        filter_scan(n)
+        copies[n].wait()
+
+        def both(b, n=n):
+            bin_block(n, b)
+            if n + 1 < scans:
+                gather(n + 1, b)
+
+        run(both)
+    out_ref[...] = sum_ref[...].astype(BF16)
+
+
+def scan_stage(scan_tiles, moved, block_tile, scan_weight, tiles, pix, strips, hots):
     slots, fields, _ = tiles.shape
-    scans, blocks = block_tile.shape
-    rows = blocks * BLK // TILE
-    width = strips.shape[2]
+    blocks = block_tile.shape[1]
     smem = pl.BlockSpec(memory_space=pltpu.SMEM)
-    whole = pl.BlockSpec((slots, fields, TILE), lambda n: (0, 0, 0))
+    vmem = pl.BlockSpec(memory_space=pltpu.VMEM)
     return pl.pallas_call(
         scan_kernel,
-        grid=(scans,),
         out_shape=jax.ShapeDtypeStruct((slots, fields, TILE), BF16),
-        in_specs=[
-            smem,
-            smem,
-            smem,
-            whole,
-            pl.BlockSpec((1, rows, TILE), lambda n: (n, 0, 0)),
-            pl.BlockSpec((1, HALF_BLK, width), lambda n: (n, 0, 0)),
-        ],
-        out_specs=whole,
+        in_specs=[smem, smem, smem, smem, vmem, vmem, vmem, pl.BlockSpec(memory_space=pl.ANY)],
+        out_specs=vmem,
         scratch_shapes=[
-            pltpu.VMEM(((2 * blocks + 4) * fields, HALF_BLK), BF16),
+            pltpu.VMEM((2, (2 * blocks + 4) * fields, HALF_BLK), BF16),
             pltpu.VMEM((2 * blocks * fields, HALF_BLK), BF16),
             pltpu.VMEM((slots, fields, TILE), F32),
-        ],
-        compiler_params=pltpu.CompilerParams(
-            vmem_limit_bytes=VMEM_LIMIT, dimension_semantics=("arbitrary",)
-        ),
+            pltpu.VMEM(hots.shape, BF16),
+            pltpu.SemaphoreType.DMA((hots.shape[0],)),
+        ],
+        compiler_params=pltpu.CompilerParams(vmem_limit_bytes=SCAN_LIMIT),
         name="scan_stage",
-    )(scan_tiles, block_tile, scan_weight, tiles, pix, strips)
+    )(scan_tiles, moved, block_tile, scan_weight, tiles, pix, strips, hots)
 
 
 def owner_kernel(position_ref, list_ref, back_ref, out_ref, owner_ref, sem, *sum_refs):
@@ -413,21 +512,31 @@
 ):
     half = lax.axis_index("half").reshape(1)
     position = lax.axis_index("dev").reshape(1)
-    devices = fetch_list.shape[0]
     fields = alm.shape[2]
-    slots = alm.shape[0]
     scans = block_pix.shape[0]
 
-    ids = order_ids.reshape(devices, slots).T
-    own, turns, table = contract_ells(ids, alm, legendre)
+    own, turns, table = contract_ells(order_ids, alm, legendre)
     other = lax.ppermute(own, "half", [(0, 1), (1, 0)])
     sent = mix_fields(half, own, other, field_mix)
+    sent, block_pix, scan_tiles = lax.optimization_barrier((sent, block_pix, scan_tiles))
     coeff = lax.all_to_all(sent, "dev", split_axis=0, concat_axis=0, tiled=True)
+    pix = block_pix.reshape(scans, -1, TILE)
+    hots = hot_blocks(pix)
+    devices, capacity = fetch_list.shape[1:]
+    source, slot = scan_tiles // capacity, scan_tiles % capacity
+    member = (source // RING) * SHARE + source % SHARE
+    moved = (member * COPIES + (source % RING) // SHARE) * capacity + slot
 
     by_slot = fetch_list.transpose(0, 2, 1)
     picked = synthesize(position, by_slot, coeff, turns, table, fields)
-    picked, noise_kernel, block_pix = lax.optimization_barrier((picked, noise_kernel, block_pix))
-    fetched = lax.all_to_all(picked, "dev", split_axis=0, concat_axis=0, tiled=True)
+    picked, noise_kernel = lax.optimization_barrier((picked, noise_kernel))
+    groups = [
+        [RING * q + SHARE * p + i for q in range(fetch_list.shape[0] // RING) for i in range(SHARE)]
+        for p in range(COPIES)
+    ]
+    fetched = lax.all_to_all(
+        picked, "dev", split_axis=0, concat_axis=0, tiled=True, axis_index_groups=groups
+    )
 
     taps = noise_kernel.astype(BF16).astype(F32)
     band = jnp.concatenate(
@@ -440,17 +549,18 @@
         axis=1,
     )
     strips = band_strips(band[:, None, :])
-    pix = block_pix.reshape(scans, -1, TILE)
     per_slot = scan_stage(
         scan_tiles,
+        moved,
         block_tile,
         scan_weight,
         fetched.reshape(-1, fields, TILE),
         pix,
         strips,
+        hots,
     )
     returned = lax.all_to_all(
-        per_slot.reshape(fetched.shape), "dev", split_axis=0, concat_axis=0, tiled=True
+        per_slot.reshape(devices, capacity, fields, TILE), "dev", split_axis=0, concat_axis=0, tiled=True
     )
     return owner_sum(position, by_slot, returned)
 

time: 124 us -> 113 us (0.911)
  waiting for transfers between devices: 41.4 us -> 19.5 us
  Pallas kernels: 22.1 us -> 28.3 us
  local copies, waits for them, and re-layouts: 1.45 us -> 7.06 us
  starting transfers between devices: 22.8 us -> 20.8 us
  blocking collectives: 35.4 us -> 37 us
    all_to_all x1, waiting for transfers between devices: 29 us -> 3.38 us  [local(): lax.all_to_all(picked, 'dev', split_axis=0, concat_axis=0, tiled=True, ax...]
    unnamed x15 -> x19, local copies, waits for them, and re-layouts: 0.05 us -> 6.51 us
    pallas_call x2 -> x3, Pallas kernels: 15.1 us -> 21 us  [the longest x1 9.42 us: scan_stage(): pl.pallas_call(scan_kernel, out_shape=jax.ShapeDtypeStruct((slots, fields...]
    all_to_all x1, waiting for transfers between devices: 11.1 us -> 14.8 us  [local(): coeff = lax.all_to_all(sent, 'dev', split_axis=0, concat_axis=0, tiled=True)]
    all_to_all x1, starting transfers between devices: 7.71 us -> 5.72 us  [local(): lax.all_to_all(picked, 'dev', split_axis=0, concat_axis=0, tiled=True, ax...]
    all_to_all x1, blocking collectives: 35.4 us -> 37 us  [local(): lax.all_to_all(per_slot.reshape(devices, capacity, fields, TILE), 'dev',...]
  transfers between devices with their start and end apart: 3 -> 3, of which waited for: 3 -> 3; matrix products, arithmetic and copies ran while one was open for 0% -> 1% of each run, Pallas kernels for 1% -> 5%
where the time goes in v3:
time: 113 us
  blocking collectives  37 us (33%)
  Pallas kernels  28.3 us (25%)
  starting transfers between devices  20.8 us (18%)
  waiting for transfers between devices  19.5 us (17%)
  local copies, waits for them, and re-layouts  7.06 us (6%)
    all_to_all x1, blocking collectives, local(): lax.all_to_all(per_slot.reshape(devices, capacity, fields, TILE), 'dev',...  37 us
    all_to_all x1, starting transfers between devices, local(): coeff = lax.all_to_all(sent, 'dev', split_axis=0, concat_axis=0, tiled=True)  15 us
    all_to_all x1, waiting for transfers between devices, local(): coeff = lax.all_to_all(sent, 'dev', split_axis=0, concat_axis=0, tiled=True)  14.8 us
    pallas_call x1, Pallas kernels, scan_stage(): pl.pallas_call(scan_kernel, out_shape=jax.ShapeDtypeStruct((slots, fields...  9.42 us
    unnamed x19, local copies, waits for them, and re-layouts  6.51 us
    pallas_call x1, Pallas kernels, synthesize(): pl.pallas_call(synth_kernel, out_shape=jax.ShapeDtypeStruct((devices // C...  6.23 us
    all_to_all x1, starting transfers between devices, local(): lax.all_to_all(picked, 'dev', split_axis=0, concat_axis=0, tiled=True, ax...  5.72 us
    pallas_call x1, Pallas kernels, hot_blocks(): pl.pallas_call(hot_kernel, grid=(scans,), out_shape=jax.ShapeDtypeStruct(...  5.32 us
  transfers between devices with their start and end apart: 3, of which 3 were waited for; matrix products, arithmetic and copies ran while one was open for 1% of the time, Pallas kernels for 5%

profile of v3, /device:TPU:32, one launch (start us, length us, event | category | flops | bytes accessed | tf_op | source)
XLA Modules:
  0.0 113.1 jit_solution(9792930195328663789)
XLA Ops:
  0.0 0.0 copy-start.2
  0.0 0.0 copy-start.1
  0.0 0.0 copy-start.4
  0.0 0.7 copy-done.4
  0.7 0.0 copy-start.7
  0.7 3.1 %contract_ells.1 = (f32[256,128]{1,0:T(8,128)S(1)}, f32[2,32,8,128]{3,2,1,0:T(8,128)S(1)}, bf16[2048,128]{1,0:T(8,128)(2,1)S(1)}) custom-call(s32[8,128]{1,0:T(8,128)S(1)} %bitcast.16, bf16[8,32,2048]{2,1,0:T(8,128)(2,1)} %bitcast.17, bf16[8,2048,128]{2,1,0:T(8,128)(2,1)} %leg_hbm.1), custom_call_target="tpu_custom_call" | custom-call | tf_op jit(solution)/shard_map/contract_ells/pallas_call | solution.py:90
  3.9 0.1 collective-permute-start
  4.0 1.3 %collective-permute-done.other_ref = f32[256,128]{1,0:T(8,128)S(1)} collective-permute-done((f32[256,128]{1,0:T(8,128)S(1)}, f32[256,128]{1,0:T(8,128)S(1)}, u32[]{:S(2)}, u32[]{:S(2)}) %collective-permute-start) | collective-permute-done | bytes 131104 | tf_op jit(solution)/shard_map/ppermute | solution.py:519
  5.3 0.0 copy-done.2
  5.3 1.7 %mix_fields.1 = bf16[128,8,128]{2,1,0:T(8,128)(2,1)} custom-call(s32[1]{0:T(128)} %bitcast.2.half_ref, f32[256,128]{1,0:T(8,128)S(1)} %get-tuple-element.13.own_ref, f32[256,128]{1,0:T(8,128)S(1)} %collective-permute-done.other_ref, f32[16,32]{1,0:T(8,128)S(1)} %copy-done.2), custom_call_target="tpu_custom_call" | custom-call | tf_op jit(solution)/shard_map/mix_fields/pallas_call | solution.py:173
  7.0 15.0 %all-to-all-start = ((bf16[128,8,128]{2,1,0:T(8,128)(2,1)}), bf16[128,8,128]{2,1,0:T(8,128)(2,1)S(1)}, u32[]{:S(2)}, u32[]{:S(2)}) async-start(bf16[128,8,128]{2,1,0:T(8,128)(2,1)} %mix_fields.1), calls=%async_computation | async-start | bytes 524288 | tf_op jit(solution)/shard_map/all_to_all | solution.py:522
  22.0 14.8 %all-to-all-done.coeff_ref = bf16[128,8,128]{2,1,0:T(8,128)(2,1)S(1)} async-done(((bf16[128,8,128]{2,1,0:T(8,128)(2,1)}), bf16[128,8,128]{2,1,0:T(8,128)(2,1)S(1)}, u32[]{:S(2)}, u32[]{:S(2)}) %all-to-all-start) | async-done | bytes 262176 | tf_op jit(solution)/shard_map/all_to_all | solution.py:522
  36.8 0.0 copy-done.1
  36.8 6.2 %synthesize.1 = bf16[32,4,2,16,128]{4,3,2,1,0:T(8,128)(2,1)} custom-call(s32[1]{0:T(128)} %bitcast.position_ref, s32[128,2,128]{2,1,0:T(2,128)S(1)} %bitcast.14, bf16[128,8,128]{2,1,0:T(8,128)(2,1)S(1)} %all-to-all-done.coeff_ref, f32[2,32,8,128]{3,2,1,0:T(8,128)S(1)} %get-tuple-element.16.turn_ref, bf16[2048,128]{1,0:T(8,128)(2,1)S(1)} %get-tuple-element.17.table_ref), custom_call_target="tpu_custom_call" | custom-call | tf_op jit(solution)/shard_map/synthesize/pallas_call | solution.py:260
  43.0 5.7 %all-to-all-start.1 = ((bf16[32,4,2,16,128]{4,3,2,1,0:T(8,128)(2,1)}), bf16[32,4,2,16,128]{4,3,2,1,0:T(8,128)(2,1)}, u32[]{:S(2)}, u32[]{:S(2)}) async-start(bf16[32,4,2,16,128]{4,3,2,1,0:T(8,128)(2,1)} %synthesize.1), calls=%async_computation.1 | async-start | bytes 2097152 | tf_op jit(solution)/shard_map/all_to_all | solution.py:537
  48.8 0.0 copy-done.7
  48.8 0.0 copy-start.3
  48.8 0.0 copy-start.8
  48.8 0.0 copy-start.5
  48.8 0.0 copy-start.6
  48.8 5.3 %hot_blocks.1.hot_hbm = bf16[4,32,512,128]{3,2,1,0:T(8,128)(2,1)S(1)} custom-call(s32[4,128,128]{2,1,0:T(8,128)S(1)} %bitcast.12), custom_call_target="tpu_custom_call" | custom-call | tf_op jit(solution)/shard_map/hot_blocks/pallas_call | solution.py:327
  54.2 0.0 copy-start
  54.2 5.7 %copy-done = bf16[4,32,512,128]{3,2,1,0:T(8,128)(2,1)} copy-done((bf16[4,32,512,128]{3,2,1,0:T(8,128)(2,1)}, bf16[4,32,512,128]{3,2,1,0:T(8,128)(2,1)S(1)}, u32[]{:S(2)}) %copy-start) | copy-done | bytes 16777240
  59.9 0.0 copy-done.3
  59.9 0.0 copy-done.8
  60.0 0.1 slice.4
  60.0 0.4 rev.3
  60.4 0.1 concatenate.3
  60.5 0.7 band_strips.1.strip_ref
  61.2 3.4 %all-to-all-done.1 = bf16[32,4,2,16,128]{4,3,2,1,0:T(8,128)(2,1)} async-done(((bf16[32,4,2,16,128]{4,3,2,1,0:T(8,128)(2,1)}), bf16[32,4,2,16,128]{4,3,2,1,0:T(8,128)(2,1)}, u32[]{:S(2)}, u32[]{:S(2)}) %all-to-all-start.1) | async-done | bytes 1048608 | tf_op jit(solution)/shard_map/all_to_all | solution.py:537
  64.6 0.0 copy-done.5
  64.6 0.0 copy-done.6
  64.6 9.4 %scan_stage.1 = bf16[256,16,128]{2,1,0:T(8,128)(2,1)S(1)} custom-call(s32[4,32]{1,0:T(4,128)S(1)} %copy-done.3, s32[4,32]{1,0:T(4,128)S(1)} %fusion.5.moved_ref, s32[4,32]{1,0:T(4,128)S(1)} %copy-done.5, f32[4]{0:T(128)S(1)} %copy-done.6, bf16[256,16,128]{2,1,0:T(8,128)(2,1)} %bitcast.5.tiles_ref, s32[4,128,128]{2,1,0:T(8,128)S(1)} %bitcast.13, ...), custom_call_target="tpu_custom_call" | custom-call | tf_op jit(solution)/shard_map/scan_stage/pallas_call | solution.py:435
  74.0 37.0 %all_to_all.15.back_ref = bf16[128,2,16,128]{3,2,1,0:T(8,128)(2,1)S(1)} all-to-all(bf16[128,2,16,128]{3,2,1,0:T(8,128)(2,1)S(1)} %bitcast.11), channel_id=1, replica_groups=mesh['half'=2,'dev'=128] {'dev'}, dimensions={0} | all-to-all | bytes 2097152 | tf_op jit(solution)/shard_map/all_to_all | solution.py:562
  111.0 1.9 %owner_sum.1 = f32[1,16,4096]{2,1,0:T(8,128)} custom-call(s32[1]{0:T(128)} %bitcast.position_ref, s32[128,2,128]{2,1,0:T(2,128)S(1)} %bitcast.15, bf16[128,2,16,128]{3,2,1,0:T(8,128)(2,1)S(1)} %all_to_all.15.back_ref), custom_call_target="tpu_custom_call" | custom-call | tf_op jit(solution)/shard_map/owner_sum/pallas_call | solution.py:483
  (6 shorter events, 0.1 us)
Async XLA Ops:
  0.0 5.3 %copy-start.2 = (f32[16,32]{1,0:T(8,128)S(1)}, f32[16,32]{1,0:T(8,128)}, u32[]{:S(2)}) copy-start(f32[16,32]{1,0:T(8,128)} %mix_ref.1) | copy-start | bytes 6148
  0.0 36.8 %copy-start.1 = (s32[128,128,2]{1,2,0:T(2,128)S(1)}, s32[128,128,2]{1,2,0:T(2,128)}, u32[]{:S(2)}) copy-start(s32[128,128,2]{1,2,0:T(2,128)} %param.14) | copy-start | bytes 393220
  0.0 0.7 copy-start.4
  0.7 48.0 %copy-start.7 = (s32[4,16384]{1,0:T(4,128)S(1)}, s32[4,16384]{1,0:T(4,128)}, u32[]{:S(2)}) copy-start(s32[4,16384]{1,0:T(4,128)} %param.17) | copy-start | bytes 786436
  3.9 1.4 %collective-permute-start = (f32[256,128]{1,0:T(8,128)S(1)}, f32[256,128]{1,0:T(8,128)S(1)}, u32[]{:S(2)}, u32[]{:S(2)}) collective-permute-start(f32[256,128]{1,0:T(8,128)S(1)} %get-tuple-element.13.own_ref), channel_id=1, source_target_pairs={{0,128},{128,0},{1,129},{129,1},{2,130},{130,2},{3,131},{131,3},{4... | collective-permute-start | bytes 393224 | tf_op jit(solution)/shard_map/ppermute | solution.py:519
  7.0 29.8 %all-to-all-start = ((bf16[128,8,128]{2,1,0:T(8,128)(2,1)}), bf16[128,8,128]{2,1,0:T(8,128)(2,1)S(1)}, u32[]{:S(2)}, u32[]{:S(2)}) async-start(bf16[128,8,128]{2,1,0:T(8,128)(2,1)} %mix_fields.1), calls=%async_computation | async-start | bytes 524288 | tf_op jit(solution)/shard_map/all_to_all | solution.py:522
  43.0 21.6 %all-to-all-start.1 = ((bf16[32,4,2,16,128]{4,3,2,1,0:T(8,128)(2,1)}), bf16[32,4,2,16,128]{4,3,2,1,0:T(8,128)(2,1)}, u32[]{:S(2)}, u32[]{:S(2)}) async-start(bf16[32,4,2,16,128]{4,3,2,1,0:T(8,128)(2,1)} %synthesize.1), calls=%async_computation.1 | async-start | bytes 2097152 | tf_op jit(solution)/shard_map/all_to_all | solution.py:537
  48.8 11.1 %copy-start.3 = (s32[4,32]{1,0:T(4,128)S(1)}, s32[4,32]{1,0:T(4,128)}, u32[]{:S(2)}) copy-start(s32[4,32]{1,0:T(4,128)} %list_ref) | copy-start | bytes 1540
  48.8 11.1 %copy-start.8 = (f32[4,512]{1,0:T(4,128)S(1)}, f32[4,512]{1,0:T(4,128)}, u32[]{:S(2)}) copy-start(f32[4,512]{1,0:T(4,128)} %param.18) | copy-start | bytes 24580
  48.8 15.8 %copy-start.5 = (s32[4,32]{1,0:T(4,128)S(1)}, s32[4,32]{1,0:T(4,128)}, u32[]{:S(2)}) copy-start(s32[4,32]{1,0:T(4,128)} %entry_ref.1) | copy-start | bytes 1540
  48.8 15.8 %copy-start.6 = (f32[4]{0:T(128)S(1)}, f32[4]{0:T(128)}, u32[]{:S(2)}) copy-start(f32[4]{0:T(128)} %weight_ref.1) | copy-start | bytes 52
  54.2 5.7 %copy-start = (bf16[4,32,512,128]{3,2,1,0:T(8,128)(2,1)}, bf16[4,32,512,128]{3,2,1,0:T(8,128)(2,1)S(1)}, u32[]{:S(2)}) copy-start(bf16[4,32,512,128]{3,2,1,0:T(8,128)(2,1)S(1)} %hot_blocks.1.hot_hbm) | copy-start | bytes 50331652

commit v4 on v3

--- a/solution.py
+++ b/solution.py
@@ -518,25 +518,15 @@
     own, turns, table = contract_ells(order_ids, alm, legendre)
     other = lax.ppermute(own, "half", [(0, 1), (1, 0)])
     sent = mix_fields(half, own, other, field_mix)
-    sent, block_pix, scan_tiles = lax.optimization_barrier((sent, block_pix, scan_tiles))
+    sent, block_pix, scan_tiles, noise_kernel = lax.optimization_barrier(
+        (sent, block_pix, scan_tiles, noise_kernel)
+    )
     coeff = lax.all_to_all(sent, "dev", split_axis=0, concat_axis=0, tiled=True)
     pix = block_pix.reshape(scans, -1, TILE)
-    hots = hot_blocks(pix)
     devices, capacity = fetch_list.shape[1:]
     source, slot = scan_tiles // capacity, scan_tiles % capacity
     member = (source // RING) * SHARE + source % SHARE
     moved = (member * COPIES + (source % RING) // SHARE) * capacity + slot
-
-    by_slot = fetch_list.transpose(0, 2, 1)
-    picked = synthesize(position, by_slot, coeff, turns, table, fields)
-    picked, noise_kernel = lax.optimization_barrier((picked, noise_kernel))
-    groups = [
-        [RING * q + SHARE * p + i for q in range(fetch_list.shape[0] // RING) for i in range(SHARE)]
-        for p in range(COPIES)
-    ]
-    fetched = lax.all_to_all(
-        picked, "dev", split_axis=0, concat_axis=0, tiled=True, axis_index_groups=groups
-    )
 
     taps = noise_kernel.astype(BF16).astype(F32)
     band = jnp.concatenate(
@@ -549,6 +539,20 @@
         axis=1,
     )
     strips = band_strips(band[:, None, :])
+    coeff, strips, pix, moved = lax.optimization_barrier((coeff, strips, pix, moved))
+
+    by_slot = fetch_list.transpose(0, 2, 1)
+    picked = synthesize(position, by_slot, coeff, turns, table, fields)
+    picked, pix = lax.optimization_barrier((picked, pix))
+    hots = hot_blocks(pix)
+    groups = [
+        [RING * q + SHARE * p + i for q in range(fetch_list.shape[0] // RING) for i in range(SHARE)]
+        for p in range(COPIES)
+    ]
+    fetched = lax.all_to_all(
+        picked, "dev", split_axis=0, concat_axis=0, tiled=True, axis_index_groups=groups
+    )
+
     per_slot = scan_stage(
         scan_tiles,
         moved,

time: 113 us -> 115 us (1.018)
  local copies, waits for them, and re-layouts: 7.06 us -> 9.86 us
    unnamed x19 -> x25, local copies, waits for them, and re-layouts: 6.51 us -> 9.31 us
    all_to_all x1, waiting for transfers between devices: 14.8 us -> 13.5 us  [local(): coeff = lax.all_to_all(sent, 'dev', split_axis=0, concat_axis=0, tiled=True)]
    all_to_all x1, waiting for transfers between devices: 3.38 us -> 4.72 us  [local(): lax.all_to_all(picked, 'dev', split_axis=0, concat_axis=0, tiled=True, ax...]
where the time goes in v4:
time: 115 us
  blocking collectives  37 us (32%)
  Pallas kernels  27.3 us (24%)
  starting transfers between devices  20.7 us (18%)
  waiting for transfers between devices  19.5 us (17%)
  local copies, waits for them, and re-layouts  9.86 us (9%)
    all_to_all x1, blocking collectives, local(): lax.all_to_all(per_slot.reshape(devices, capacity, fields, TILE), 'dev',...  37 us
    all_to_all x1, starting transfers between devices, local(): coeff = lax.all_to_all(sent, 'dev', split_axis=0, concat_axis=0, tiled=True)  15 us
    all_to_all x1, waiting for transfers between devices, local(): coeff = lax.all_to_all(sent, 'dev', split_axis=0, concat_axis=0, tiled=True)  13.5 us
    pallas_call x1, Pallas kernels, scan_stage(): pl.pallas_call(scan_kernel, out_shape=jax.ShapeDtypeStruct((slots, fields...  9.41 us
    unnamed x25, local copies, waits for them, and re-layouts  9.31 us
    all_to_all x1, starting transfers between devices, local(): lax.all_to_all(picked, 'dev', split_axis=0, concat_axis=0, tiled=True, ax...  5.72 us
    pallas_call x1, Pallas kernels, hot_blocks(): pl.pallas_call(hot_kernel, grid=(scans,), out_shape=jax.ShapeDtypeStruct(...  5.32 us
    pallas_call x1, Pallas kernels, synthesize(): pl.pallas_call(synth_kernel, out_shape=jax.ShapeDtypeStruct((devices // C...  5.22 us
  transfers between devices with their start and end apart: 3, of which 3 were waited for; matrix products, arithmetic and copies ran while one was open for 1% of the time, Pallas kernels for 5%

profile of v4, /device:TPU:32, one launch (start us, length us, event | category | flops | bytes accessed | tf_op | source)
XLA Modules:
  0.0 114.8 jit_solution(1322803775520486618)
XLA Ops:
  0.0 0.0 copy-start.5
  0.0 0.0 copy-start.7
  0.0 0.7 copy-done.7
  0.7 0.0 copy-start.11
  0.7 0.0 copy-start.10
  0.7 0.0 copy-start.6
  0.7 0.0 copy-start.4
  0.7 3.1 %contract_ells.1 = (f32[256,128]{1,0:T(8,128)S(1)}, f32[2,32,8,128]{3,2,1,0:T(8,128)S(1)}, bf16[2048,128]{1,0:T(8,128)(2,1)S(1)}) custom-call(s32[8,128]{1,0:T(8,128)S(1)} %bitcast.16, bf16[8,32,2048]{2,1,0:T(8,128)(2,1)} %bitcast.17, bf16[8,2048,128]{2,1,0:T(8,128)(2,1)} %leg_hbm.1), custom_call_target="tpu_custom_call" | custom-call | tf_op jit(solution)/shard_map/contract_ells/pallas_call | solution.py:90
  3.9 0.0 copy-start.2
  3.9 0.8 copy-done.2
  4.7 0.0 collective-permute-start
  4.7 1.3 %collective-permute-done.other_ref = f32[256,128]{1,0:T(8,128)S(1)} collective-permute-done((f32[256,128]{1,0:T(8,128)S(1)}, f32[256,128]{1,0:T(8,128)S(1)}, u32[]{:S(2)}, u32[]{:S(2)}) %collective-permute-start) | collective-permute-done | bytes 131104 | tf_op jit(solution)/shard_map/ppermute | solution.py:519
  6.0 0.0 copy-done.5
  6.0 1.7 %mix_fields.1 = bf16[128,8,128]{2,1,0:T(8,128)(2,1)} custom-call(s32[1]{0:T(128)} %bitcast.2.half_ref, f32[256,128]{1,0:T(8,128)S(1)} %get-tuple-element.18.own_ref, f32[256,128]{1,0:T(8,128)S(1)} %collective-permute-done.other_ref, f32[16,32]{1,0:T(8,128)S(1)} %copy-done.5), custom_call_target="tpu_custom_call" | custom-call | tf_op jit(solution)/shard_map/mix_fields/pallas_call | solution.py:173
  7.7 15.0 %all-to-all-start = ((bf16[128,8,128]{2,1,0:T(8,128)(2,1)}), bf16[128,8,128]{2,1,0:T(8,128)(2,1)S(1)}, u32[]{:S(2)}, u32[]{:S(2)}) async-start(bf16[128,8,128]{2,1,0:T(8,128)(2,1)} %mix_fields.1), calls=%async_computation | async-start | bytes 524288 | tf_op jit(solution)/shard_map/all_to_all | solution.py:524
  22.7 0.0 copy-done.11
  22.7 0.1 slice.4
  22.8 0.4 rev.3
  23.1 0.1 concatenate.3
  23.3 0.0 copy-done.10
  23.3 0.7 band_strips.1.strip_ref
  24.0 0.0 copy-done.6
  24.0 13.5 %all-to-all-done.coeff_ref = bf16[128,8,128]{2,1,0:T(8,128)(2,1)S(1)} async-done(((bf16[128,8,128]{2,1,0:T(8,128)(2,1)}), bf16[128,8,128]{2,1,0:T(8,128)(2,1)S(1)}, u32[]{:S(2)}, u32[]{:S(2)}) %all-to-all-start) | async-done | bytes 262176 | tf_op jit(solution)/shard_map/all_to_all | solution.py:524
  37.5 0.0 copy-done.4
  37.5 0.0 copy-start.3
  37.5 1.0 copy-done.3
  38.5 5.2 %synthesize.1 = bf16[32,4,2,16,128]{4,3,2,1,0:T(8,128)(2,1)S(1)} custom-call(s32[1]{0:T(128)} %bitcast.position_ref, s32[128,2,128]{2,1,0:T(2,128)S(1)} %bitcast.14, bf16[128,8,128]{2,1,0:T(8,128)(2,1)S(1)} %all-to-all-done.coeff_ref, f32[2,32,8,128]{3,2,1,0:T(8,128)S(1)} %get-tuple-element.25.turn_ref, bf16[2048,128]{1,0:T(8,128)(2,1)S(1)} %copy-done.3), custom_call_target="tpu_custom_call" | custom-call | tf_op jit(solution)/shard_map/synthesize/pallas_call | solution.py:260
  43.8 0.0 copy-start.1
  43.8 1.0 copy-done.1
  44.8 5.7 %all-to-all-start.1 = ((bf16[32,4,2,16,128]{4,3,2,1,0:T(8,128)(2,1)}), bf16[32,4,2,16,128]{4,3,2,1,0:T(8,128)(2,1)}, u32[]{:S(2)}, u32[]{:S(2)}) async-start(bf16[32,4,2,16,128]{4,3,2,1,0:T(8,128)(2,1)} %copy-done.1), calls=%async_computation.1 | async-start | bytes 2097152 | tf_op jit(solution)/shard_map/all_to_all | solution.py:552
  50.5 0.0 copy-start.8
  50.5 0.0 copy-start.9
  50.5 5.3 %hot_blocks.1.hot_hbm = bf16[4,32,512,128]{3,2,1,0:T(8,128)(2,1)S(1)} custom-call(s32[4,128,128]{2,1,0:T(8,128)S(1)} %bitcast.12), custom_call_target="tpu_custom_call" | custom-call | tf_op jit(solution)/shard_map/hot_blocks/pallas_call | solution.py:327
  55.9 0.0 copy-start
  55.9 5.7 %copy-done = bf16[4,32,512,128]{3,2,1,0:T(8,128)(2,1)} copy-done((bf16[4,32,512,128]{3,2,1,0:T(8,128)(2,1)}, bf16[4,32,512,128]{3,2,1,0:T(8,128)(2,1)S(1)}, u32[]{:S(2)}) %copy-start) | copy-done | bytes 16777240
  61.6 4.7 %all-to-all-done.1 = bf16[32,4,2,16,128]{4,3,2,1,0:T(8,128)(2,1)} async-done(((bf16[32,4,2,16,128]{4,3,2,1,0:T(8,128)(2,1)}), bf16[32,4,2,16,128]{4,3,2,1,0:T(8,128)(2,1)}, u32[]{:S(2)}, u32[]{:S(2)}) %all-to-all-start.1) | async-done | bytes 1048608 | tf_op jit(solution)/shard_map/all_to_all | solution.py:552
  66.3 0.0 copy-done.8
  66.3 0.0 copy-done.9
  66.3 9.4 %scan_stage.1 = bf16[256,16,128]{2,1,0:T(8,128)(2,1)S(1)} custom-call(s32[4,32]{1,0:T(4,128)S(1)} %copy-done.6, s32[4,32]{1,0:T(4,128)S(1)} %fusion.5.moved_ref, s32[4,32]{1,0:T(4,128)S(1)} %copy-done.8, f32[4]{0:T(128)S(1)} %copy-done.9, bf16[256,16,128]{2,1,0:T(8,128)(2,1)} %bitcast.5.tiles_ref, s32[4,128,128]{2,1,0:T(8,128)S(1)} %bitcast.13, ...), custom_call_target="tpu_custom_call" | custom-call | tf_op jit(solution)/shard_map/scan_stage/pallas_call | solution.py:435
  75.8 37.0 %all_to_all.15.back_ref = bf16[128,2,16,128]{3,2,1,0:T(8,128)(2,1)S(1)} all-to-all(bf16[128,2,16,128]{3,2,1,0:T(8,128)(2,1)S(1)} %bitcast.11), channel_id=1, replica_groups=mesh['half'=2,'dev'=128] {'dev'}, dimensions={0} | all-to-all | bytes 2097152 | tf_op jit(solution)/shard_map/all_to_all | solution.py:566
  112.8 1.9 %owner_sum.1 = f32[1,16,4096]{2,1,0:T(8,128)} custom-call(s32[1]{0:T(128)} %bitcast.position_ref, s32[128,2,128]{2,1,0:T(2,128)S(1)} %bitcast.15, bf16[128,2,16,128]{3,2,1,0:T(8,128)(2,1)S(1)} %all_to_all.15.back_ref), custom_call_target="tpu_custom_call" | custom-call | tf_op jit(solution)/shard_map/owner_sum/pallas_call | solution.py:483
  (6 shorter events, 0.1 us)
Async XLA Ops:
  0.0 6.0 %copy-start.5 = (f32[16,32]{1,0:T(8,128)S(1)}, f32[16,32]{1,0:T(8,128)}, u32[]{:S(2)}) copy-start(f32[16,32]{1,0:T(8,128)} %mix_ref.1) | copy-start | bytes 6148
  0.0 0.7 copy-start.7
  0.7 22.0 %copy-start.11 = (f32[4,512]{1,0:T(4,128)S(1)}, f32[4,512]{1,0:T(4,128)}, u32[]{:S(2)}) copy-start(f32[4,512]{1,0:T(4,128)} %param.18) | copy-start | bytes 24580
  0.7 22.6 %copy-start.10 = (s32[4,16384]{1,0:T(4,128)S(1)}, s32[4,16384]{1,0:T(4,128)}, u32[]{:S(2)}) copy-start(s32[4,16384]{1,0:T(4,128)} %param.17) | copy-start | bytes 786436
  0.7 23.3 %copy-start.6 = (s32[4,32]{1,0:T(4,128)S(1)}, s32[4,32]{1,0:T(4,128)}, u32[]{:S(2)}) copy-start(s32[4,32]{1,0:T(4,128)} %list_ref) | copy-start | bytes 1540
  0.7 36.8 %copy-start.4 = (s32[128,128,2]{1,2,0:T(2,128)S(1)}, s32[128,128,2]{1,2,0:T(2,128)}, u32[]{:S(2)}) copy-start(s32[128,128,2]{1,2,0:T(2,128)} %param.14) | copy-start | bytes 393220
  3.9 0.8 copy-start.2
  4.7 1.3 %collective-permute-start = (f32[256,128]{1,0:T(8,128)S(1)}, f32[256,128]{1,0:T(8,128)S(1)}, u32[]{:S(2)}, u32[]{:S(2)}) collective-permute-start(f32[256,128]{1,0:T(8,128)S(1)} %get-tuple-element.18.own_ref), channel_id=1, source_target_pairs={{0,128},{128,0},{1,129},{129,1},{2,130},{130,2},{3,131},{131,3},{4... | collective-permute-start | bytes 393224 | tf_op jit(solution)/shard_map/ppermute | solution.py:519
  7.7 29.8 %all-to-all-start = ((bf16[128,8,128]{2,1,0:T(8,128)(2,1)}), bf16[128,8,128]{2,1,0:T(8,128)(2,1)S(1)}, u32[]{:S(2)}, u32[]{:S(2)}) async-start(bf16[128,8,128]{2,1,0:T(8,128)(2,1)} %mix_fields.1), calls=%async_computation | async-start | bytes 524288 | tf_op jit(solution)/shard_map/all_to_all | solution.py:524
  37.5 1.0 copy-start.3
  43.8 1.0 copy-start.1
  44.8 21.6 %all-to-all-start.1 = ((bf16[32,4,2,16,128]{4,3,2,1,0:T(8,128)(2,1)}), bf16[32,4,2,16,128]{4,3,2,1,0:T(8,128)(2,1)}, u32[]{:S(2)}, u32[]{:S(2)}) async-start(bf16[32,4,2,16,128]{4,3,2,1,0:T(8,128)(2,1)} %copy-done.1), calls=%async_computation.1 | async-start | bytes 2097152 | tf_op jit(solution)/shard_map/all_to_all | solution.py:552
  50.5 15.8 %copy-start.8 = (s32[4,32]{1,0:T(4,128)S(1)}, s32[4,32]{1,0:T(4,128)}, u32[]{:S(2)}) copy-start(s32[4,32]{1,0:T(4,128)} %entry_ref.1) | copy-start | bytes 1540
  50.5 15.8 %copy-start.9 = (f32[4]{0:T(128)S(1)}, f32[4]{0:T(128)}, u32[]{:S(2)}) copy-start(f32[4]{0:T(128)} %weight_ref.1) | copy-start | bytes 52
  55.9 5.7 %copy-start = (bf16[4,32,512,128]{3,2,1,0:T(8,128)(2,1)}, bf16[4,32,512,128]{3,2,1,0:T(8,128)(2,1)S(1)}, u32[]{:S(2)}) copy-start(bf16[4,32,512,128]{3,2,1,0:T(8,128)(2,1)S(1)} %hot_blocks.1.hot_hbm) | copy-start | bytes 50331652
